TPU v7x, 512 devices: a whole 4x8x8 slice. The times are simulated.
512 devices in a mesh: seq: 16 (over y_lo, z), clus: 32 (over x, y_hi, core).
Axes of the slice: x: 4, y: 8 (y_hi: 4, y_lo: 2; y = y_hi * 2 + y_lo), z: 8, core: 2. Of those that a mesh axis runs over, the one named last changes fastest.
Arguments:
- node_feats: bfloat16 [32, 2048, 1024], P('clus', 'seq'), may hold values from -24 to 24
- qkv_weight: bfloat16 [3072, 1024], P('seq'), may hold values from -1 to 1
- block_pairs: int32 [32, 128, 2], P('clus'), may hold values from 0 to 15, as said below
- grad_out: bfloat16 [32, 2048, 1024], P('clus', 'seq'), may hold values from -6 to 6
Outputs:
- attended: bfloat16 [32, 2048, 1024], P('clus', 'seq')
- node_grad: bfloat16 [32, 2048, 1024], P('clus', 'seq')
- weight_grad: float32 [3072, 1024], P('seq')
Inputs may be any that keep to these rules, and one draw needn't show every extreme that they name: `block_pairs`: each cluster's list holds 128 distinct pairs, among them (b, b) for every block b.
All inputs are finite; a program needn't handle non-finite values.
Results may differ from a plain program's by a relative error of at most 0.023.
Values may be sent and summed in bfloat16 or wider, within the bound.
A program may use at most 64 MiB of HBM per device.

v0:
```python
import math

import jax
import jax.numpy as jnp
from jax import lax
from jax.sharding import PartitionSpec as P

HD = 64
BLOCK = 128


def block_allowed(listed, blocks):
    block_ids = jnp.arange(blocks, dtype=jnp.int32)[None, :]
    row_hot = (listed[:, 0:1] == block_ids).astype(jnp.float32)
    col_hot = (listed[:, 1:2] == block_ids).astype(jnp.float32)
    counts = jnp.dot(row_hot.T, col_hot, precision=lax.Precision.HIGHEST)
    return counts > 0.5


def expand_rows(allowed_blocks, offset, row_span):
    picked = lax.dynamic_slice_in_dim(allowed_blocks, offset // BLOCK, row_span // BLOCK, 0)
    return jnp.repeat(jnp.repeat(picked, BLOCK, axis=0), BLOCK, axis=1)


def softmax_rows(query_rows, keys_all, allowed_rows):
    scores = jnp.einsum(
        "qhe,khe->hqk", query_rows, keys_all, preferred_element_type=jnp.float32
    ) * HD ** (-0.5)
    scores = jnp.where(allowed_rows[None], scores, -jnp.inf)
    row_max = jnp.max(scores, axis=-1, keepdims=True)
    unnorm = jnp.where(allowed_rows[None], jnp.exp(scores - row_max), 0.0)
    return unnorm / jnp.sum(unnorm, axis=-1, keepdims=True)


def local(node_feats, qkv_weight, block_pairs, grad_out):
    features = node_feats[0]
    rows_dev = features.shape[0]
    node_count = rows_dev * lax.axis_size("seq")
    columns = qkv_weight.shape[0]
    heads_dev = columns // (3 * HD)
    row_span = math.gcd(node_count, 512)
    offsets = jnp.arange(node_count // row_span, dtype=jnp.int32) * row_span
    projected = lax.dot_general(
        lax.all_gather(features, "seq", axis=0, tiled=True),
        qkv_weight,
        (((1,), (1,)), ((), ())),
        preferred_element_type=jnp.float32,
    ).astype(jnp.bfloat16)
    grouped = projected.reshape(node_count, heads_dev, 3, HD)
    queries = grouped[:, :, 0]
    keys_all = grouped[:, :, 1]
    values_all = grouped[:, :, 2]
    allowed_blocks = block_allowed(block_pairs[0], node_count // BLOCK)

    def forward_block(offset):
        query_rows = lax.dynamic_slice_in_dim(queries, offset, row_span, 0)
        weights = softmax_rows(query_rows, keys_all, expand_rows(allowed_blocks, offset, row_span))
        return jnp.einsum(
            "hqk,khe->qhe",
            weights.astype(jnp.bfloat16),
            values_all,
            preferred_element_type=jnp.float32,
        ).astype(jnp.bfloat16)

    head_out = lax.map(forward_block, offsets).reshape(node_count, heads_dev * HD)
    attended = lax.all_to_all(head_out, "seq", split_axis=0, concat_axis=1, tiled=True)
    upstream = lax.all_to_all(grad_out[0], "seq", split_axis=1, concat_axis=0, tiled=True).reshape(
        node_count, heads_dev, HD
    )

    def backward_block(state_pair, offset):
        grad_keys, grad_values = state_pair
        query_rows = lax.dynamic_slice_in_dim(queries, offset, row_span, 0)
        grad_rows = lax.dynamic_slice_in_dim(upstream, offset, row_span, 0)
        weights = softmax_rows(query_rows, keys_all, expand_rows(allowed_blocks, offset, row_span))
        weights_low = weights.astype(jnp.bfloat16)
        grad_weights = jnp.einsum(
            "qhe,khe->hqk", grad_rows, values_all, preferred_element_type=jnp.float32
        )
        row_delta = jnp.sum(weights * grad_weights, axis=-1, keepdims=True)
        grad_scores = (weights * (grad_weights - row_delta) * HD ** (-0.5)).astype(jnp.bfloat16)
        grad_query = jnp.einsum(
            "hqk,khe->qhe", grad_scores, keys_all, preferred_element_type=jnp.float32
        ).astype(jnp.bfloat16)
        grad_keys = grad_keys + jnp.einsum(
            "hqk,qhe->khe", grad_scores, query_rows, preferred_element_type=jnp.float32
        )
        grad_values = grad_values + jnp.einsum(
            "hqk,qhe->khe", weights_low, grad_rows, preferred_element_type=jnp.float32
        )
        return ((grad_keys, grad_values), grad_query)

    zeros_acc = jnp.zeros((node_count, heads_dev, HD), jnp.float32)
    sums_pair, grad_query = lax.scan(backward_block, (zeros_acc, zeros_acc), offsets)
    grad_query = grad_query.reshape(node_count, heads_dev, HD)
    grad_proj = jnp.stack(
        [grad_query, sums_pair[0].astype(jnp.bfloat16), sums_pair[1].astype(jnp.bfloat16)], axis=2
    ).reshape(node_count, columns)
    rows_part = grad_proj
    node_grad = lax.psum_scatter(
        jnp.dot(rows_part, qkv_weight, preferred_element_type=jnp.float32).astype(jnp.bfloat16),
        "seq",
        scatter_dimension=0,
        tiled=True,
    )
    rows_part = grad_proj
    local_sum = lax.dot_general(
        rows_part,
        lax.all_gather(features, "seq", axis=0, tiled=True),
        (((0,), (0,)), ((), ())),
        preferred_element_type=jnp.float32,
    )
    weight_grad = lax.psum(local_sum.astype(jnp.bfloat16), "clus").astype(
        jnp.float32
    ) / lax.axis_size("clus")
    return (attended[None], node_grad[None], weight_grad)


def solution(mesh):
    return jax.shard_map(
        local,
        mesh=mesh,
        in_specs=(
            P("clus", "seq", None),
            P("seq", None),
            P("clus", None, None),
            P("clus", "seq", None),
        ),
        out_specs=(P("clus", "seq", None), P("clus", "seq", None), P("seq", None)),
        check_vma=False,
    )
```

profile of v0, /device:TPU:6, one launch (start us, length us, event | category | flops | bytes accessed | tf_op | source)
XLA Modules:
  0.0 562.7 jit_solution(15509004296155294109)
XLA Ops:
  9.7 11.4 %all-to-all-start.1 = ((bf16[128,16,64]{0,2,1:T(8,128)(2,1)}), bf16[128,16,64]{0,2,1:T(8,128)(2,1)S(1)}, u32[]{:S(2)}, u32[]{:S(2)}) async-start(bf16[128,16,64]{0,2,1:T(8,128)(2,1)} %bitcast.19), calls=%async_computation.1 | async-start | bytes 524288 | tf_op jit(solution)/shard_map/all_to_all | solution.py:67
  22.2 9.6 %all-to-all-done.1 = bf16[128,16,64]{0,2,1:T(8,128)(2,1)S(1)} async-done(((bf16[128,16,64]{0,2,1:T(8,128)(2,1)}), bf16[128,16,64]{0,2,1:T(8,128)(2,1)S(1)}, u32[]{:S(2)}, u32[]{:S(2)}) %all-to-all-start.1) | async-done | bytes 262176 | tf_op jit(solution)/shard_map/all_to_all | solution.py:67
  32.8 61.0 %all-gather.3.cloned.1.call-done = bf16[1,2048,1024]{2,1,0:T(8,128)(2,1)} async-done(((bf16[1,128,1024]{2,1,0:T(8,128)(2,1)}), bf16[1,2048,1024]{2,1,0:T(8,128)(2,1)}) %all-gather.3.cloned.1.call-update) | async-done | bytes 4194320 | tf_op jit(solution)/shard_map/all_gather | solution.py:44
  93.8 3.7 fusion.44
  99.2 88.3 %while.30 = (s32[]{:T(128)}, f32[2048,1,64]{0,2,1:T(8,128)S(1)}, f32[2048,1,64]{0,2,1:T(8,128)S(1)}, bf16[4,512,1,64]{1,3,2,0:T(8,128)(2,1)}, s32[4]{0:T(128)S(1...) while((s32[]{:T(128)}, f32[2048,1,64]{0,2,1:T(8,128)S(1)}, ...), condition=%wide.region_8.9_spmd.clone, body=%wide.region_4.8_spmd.clone.sunk | while | flops 692615680 | bytes 80837776 | solution.py:94
  102.1 3.5 broadcast_in_dim.122
  110.2 3.0 multiply_reduce_fusion.2
  124.2 3.5 broadcast_in_dim.122
  132.3 3.0 multiply_reduce_fusion.2
  146.3 3.5 broadcast_in_dim.122
  154.4 3.0 multiply_reduce_fusion.2
  168.4 3.5 broadcast_in_dim.122
  176.5 3.0 multiply_reduce_fusion.2
  189.0 3.9 fusion.47
  193.2 3.2 convolution_convert_fusion.1
  196.5 56.6 %while.29 = (s32[]{:T(128)}, bf16[4,512,1,64]{1,3,2,0:T(8,128)(2,1)S(1)}, s32[4]{0:T(128)S(1)}, pred[16,16]{1,0:T(8,128)(4,1)S(1)}, bf16[2048,1,64]{0,2,1:T(8,12...) while((s32[]{:T(128)}, ...), condition=%wide.region_3.4_spmd, body=%wide.region_0.3_spmd.sunk | while | flops 283147264 | bytes 17459756 | solution.py:65
  199.8 3.5 broadcast_in_dim.117
  213.9 3.5 broadcast_in_dim.117
  228.1 3.5 broadcast_in_dim.117
  236.4 2.6 fusion.77
  242.2 3.5 broadcast_in_dim.117
  254.2 3.9 all-to-all-start
  258.1 203.0 %all-reduce.2.cloned.1.call-done = bf16[192,1024]{1,0:T(8,128)(2,1)} async-done(((bf16[192,1024]{1,0:T(8,128)(2,1)}), bf16[192,1024]{1,0:T(8,128)(2,1)}) %all-reduce.2.cloned.1.call-update) | async-done | bytes 393232 | tf_op jit(solution)/shard_map/psum | solution.py:113
  463.9 92.3 %reduce-scatter.2.cloned.1.call-done = bf16[128,1024]{1,0:T(8,128)(2,1)} async-done(((bf16[2048,1024]{1,0:T(8,128)(2,1)}), bf16[128,1024]{1,0:T(8,128)(2,1)}) %reduce-scatter.2.cloned.1.call-update) | async-done | bytes 262160 | tf_op jit(solution)/shard_map/reduce_scatter | solution.py:100
  (104 shorter events, 85.1 us)
Async XLA Ops:
  7.2 86.7 %copy-start = (bf16[192,1024]{1,0:T(8,128)(2,1)S(1)}, bf16[192,1024]{1,0:T(8,128)(2,1)}, u32[]{:S(2)}) copy-start(bf16[192,1024]{1,0:T(8,128)(2,1)} %param.9) | copy-start | bytes 1179652
  7.2 86.7 %all-gather.3.cloned.1.call-start = ((), (), s32[]{:S(2)}) async-start(), calls=%async_computation.5 | async-start | bytes 4456448 | tf_op jit(solution)/shard_map/all_gather | solution.py:44
  9.7 22.1 %all-to-all-start.1 = ((bf16[128,16,64]{0,2,1:T(8,128)(2,1)}), bf16[128,16,64]{0,2,1:T(8,128)(2,1)S(1)}, u32[]{:S(2)}, u32[]{:S(2)}) async-start(bf16[128,16,64]{0,2,1:T(8,128)(2,1)} %bitcast.19), calls=%async_computation.1 | async-start | bytes 524288 | tf_op jit(solution)/shard_map/all_to_all | solution.py:67
  21.1 439.9 %all-reduce.2.cloned.1.call-start = ((), (), s32[]{:S(2)}) async-start(), calls=%async_computation.4 | async-start | bytes 786432 | tf_op jit(solution)/shard_map/psum | solution.py:113
  113.3 2.0 copy-start.1
  115.8 4.0 copy-start.2
  135.4 2.0 copy-start.1
  137.9 4.0 copy-start.2
  157.5 2.0 copy-start.1
  160.0 4.0 copy-start.2
  179.6 2.0 copy-start.1
  182.1 4.0 copy-start.2
  192.9 363.3 %reduce-scatter.2.cloned.1.call-start = ((), (), s32[]{:S(2)}) async-start(), calls=%async_computation.3 | async-start | bytes 4456448 | tf_op jit(solution)/shard_map/reduce_scatter | solution.py:100
  254.2 208.8 %all-to-all-start = ((bf16[16,128,64]{1,2,0:T(8,128)(2,1)}), bf16[16,128,64]{1,2,0:T(8,128)(2,1)S(1)}, u32[]{:S(2)}, u32[]{:S(2)}) async-start(bf16[16,128,64]{1,2,0:T(8,128)(2,1)} %copy.18), calls=%async_computation | async-start | bytes 524288 | tf_op jit(solution)/shard_map/all_to_all | solution.py:66
Sparse Core Ops, SparseCore 0:
  10.1 83.7 all-gather.2
  193.1 267.9 all-reduce.1
  464.5 91.6 reduce-scatter.1
where the time goes:
time: 564 us; the launch traced here: 563 us
  waiting for transfers between devices  367 us (65%)
  matrix products  72.6 us (13%)
  local copies, waits for them, and re-layouts  49.3 us (9%)
  loops' own time  29.3 us (5%)
  starting transfers between devices  15.6 us (3%)
  other arithmetic  15.5 us (3%)
  between operations  13.9 us (2%)
    psum x1, waiting for transfers between devices, local(): lax.psum(local_sum.astype(jnp.bfloat16), 'clus').astype(jnp.float32)  203 us
    reduce_scatter x1, waiting for transfers between devices, local(): lax.psum_scatter(jnp.dot(rows_part, qkv_weight, preferred_element_type=jn...  92.3 us
    all_gather x1, waiting for transfers between devices, local(): lax.all_gather(features, 'seq', axis=0, tiled=True)  61 us
    broadcast_in_dim x16, local copies, waits for them, and re-layouts, expand_rows(): return jnp.repeat(jnp.repeat(picked, BLOCK, axis=0), BLOCK, axis=1)  27.9 us
    dot_general x8, matrix products, softmax_rows(): jnp.einsum('qhe,khe->hqk', query_rows, keys_all, preferred_element_type=j...  17.3 us
    another operation x1, loops' own time, local(): lax.map(forward_block, offsets).reshape(node_count, heads_dev * HD)  15.5 us
    another operation x1, loops' own time, local(): lax.scan(backward_block, (zeros_acc, zeros_acc), offsets)  13.8 us
    dot_general x4, matrix products, backward_block(): jnp.einsum('qhe,khe->hqk', grad_rows, values_all, preferred_element_type=...  12.1 us
  transfers between devices with their start and end apart: 5, of which 4 were waited for; matrix products, arithmetic and copies ran while one was open for 9% of the time, Pallas kernels for 0%

commit v1 on v0

v1 whole, which is shorter than its diff:
```python
import jax
import jax.numpy as jnp
from jax import lax
from jax.experimental import pallas as pl
from jax.experimental.pallas import tpu as pltpu
from jax.sharding import PartitionSpec as P

F32 = jnp.float32
BF = jnp.bfloat16
HD = 64
BLOCK = 128
NB = 16
CH = 4
ROWS = CH * BLOCK
PAD = -1e30


def attn_kernel(pairs, b1, b2, kv, kvt, ot, dproj, cols, cnt, s_scr, d_scr, acc):
    npairs = pairs.shape[0] // 2

    def clear(t, _):
        cols[t] = 0
        return 0

    lax.fori_loop(0, NB * NB, clear, 0)

    def clear_cnt(t, _):
        cnt[t] = 0
        return 0

    lax.fori_loop(0, NB, clear_cnt, 0)

    def put(t, _):
        r = pairs[2 * t]
        n = cnt[r]
        cols[r * NB + n] = pairs[2 * t + 1]
        cnt[r] = n + 1
        return 0

    lax.fori_loop(0, npairs, put, 0)
    acc[...] = jnp.zeros_like(acc)

    def row(i, _):
        n = cnt[i]
        nch = (n + CH - 1) // CH
        w1 = b1[i]
        w2 = b2[i]

        def pass1(c, m):
            for t in range(CH):
                slot = c * CH + t
                j = cols[i * NB + slot]
                blk = kv[pl.ds(pl.multiple_of(j * BLOCK, BLOCK), BLOCK), :]
                sd = jnp.dot(blk, w1, preferred_element_type=F32)
                bias = jnp.where(slot < n, 0.0, PAD).astype(F32)
                s = sd[:, :BLOCK] + bias
                at = pl.ds(pl.multiple_of(slot * BLOCK, BLOCK), BLOCK)
                s_scr[at, :] = s
                d_scr[at, :] = sd[:, BLOCK:]
                m = jnp.maximum(m, jnp.max(s.reshape(16, 8, BLOCK), axis=0))
            return m

        m = lax.fori_loop(0, nch, pass1, jnp.full((8, BLOCK), PAD, F32))
        m = jnp.max(m, axis=0, keepdims=True)

        def pass2(c, carry):
            l, d = carry
            at = pl.ds(pl.multiple_of(c * ROWS, ROWS), ROWS)
            e = jnp.exp((s_scr[at, :] - m) * 0.125)
            s_scr[at, :] = e
            l = l + jnp.sum(e.reshape(ROWS // 8, 8, BLOCK), axis=0)
            d = d + jnp.sum((e * d_scr[at, :]).reshape(ROWS // 8, 8, BLOCK), axis=0)
            return l, d

        zero = jnp.zeros((8, BLOCK), F32)
        l, d = lax.fori_loop(0, nch, pass2, (zero, zero))
        linv = 1.0 / jnp.sum(l, axis=0, keepdims=True)
        delta = jnp.sum(d, axis=0, keepdims=True) * linv
        lscale = linv * 0.125

        def pass3(c, oq):
            at = pl.ds(pl.multiple_of(c * ROWS, ROWS), ROWS)
            e = s_scr[at, :]
            p = (e * linv).astype(BF)
            ds = (e * lscale * (d_scr[at, :] - delta)).astype(BF)
            cat = jnp.concatenate([ds, p], axis=1)
            lhs = jnp.concatenate(
                [
                    kvt[:, pl.ds(pl.multiple_of(cols[i * NB + c * CH + t] * BLOCK, BLOCK), BLOCK)]
                    for t in range(CH)
                ],
                axis=1,
            )
            oq = oq + jnp.dot(lhs, cat, preferred_element_type=F32)
            g = jnp.dot(cat, w2, preferred_element_type=F32)
            for t in range(CH):
                j = cols[i * NB + c * CH + t]
                aj = pl.ds(pl.multiple_of(j * BLOCK, BLOCK), BLOCK)
                acc[aj, :] += g[t * BLOCK : (t + 1) * BLOCK]
            return oq

        oq = lax.fori_loop(0, nch, pass3, jnp.zeros((BLOCK, 2 * BLOCK), F32))
        here = pl.ds(pl.multiple_of(i * BLOCK, BLOCK), BLOCK)
        ot[i] = oq[HD:, BLOCK:].astype(BF)
        dproj[here, 0:BLOCK] = oq[:, :BLOCK].T.astype(BF)
        return 0

    lax.fori_loop(0, NB, row, 0)

    def fin(i, _):
        here = pl.ds(pl.multiple_of(i * BLOCK, BLOCK), BLOCK)
        a = acc[here, :].astype(BF)
        q = dproj[here, 0:BLOCK]
        dproj[here, :] = jnp.concatenate([q[:, :HD], a], axis=1)
        return 0

    lax.fori_loop(0, NB, fin, 0)


def attention(pairs, b1, b2, kv, kvt):
    vm = pl.BlockSpec(memory_space=pltpu.VMEM)
    n = kv.shape[0]
    return pl.pallas_call(
        attn_kernel,
        out_shape=(
            jax.ShapeDtypeStruct((NB, HD, BLOCK), BF),
            jax.ShapeDtypeStruct((n, 3 * HD), BF),
        ),
        in_specs=[pl.BlockSpec(memory_space=pltpu.SMEM), vm, vm, vm, vm],
        out_specs=(vm, vm),
        scratch_shapes=[
            pltpu.SMEM((NB * NB,), jnp.int32),
            pltpu.SMEM((NB,), jnp.int32),
            pltpu.VMEM((n, BLOCK), F32),
            pltpu.VMEM((n, BLOCK), F32),
            pltpu.VMEM((n, BLOCK), F32),
        ],
        compiler_params=pltpu.CompilerParams(vmem_limit_bytes=40 * 1024 * 1024),
        name="attention",
    )(pairs, b1, b2, kv, kvt)

MESH = pl.DeviceIdType.MESH
HD = 64
BLOCK = 128
NB = 16
NZ = 8
D = 1024
HALF = 64
QUART = 32
CORES = 2
NX = 4
NY = 4


def dot_t(a, b):
    return lax.dot_general(a, b, (((1,), (1,)), ((), ())), preferred_element_type=F32)


def ring_place():
    s = lax.axis_index("seq")
    y = lax.div(s, NZ)
    z = lax.rem(s, NZ)
    return s, y, z


def greet(peers):
    barrier = pltpu.get_barrier_semaphore()
    for peer in peers:
        pl.semaphore_signal(barrier, inc=1, device_id=peer, device_id_type=MESH)
    pl.semaphore_wait(barrier, len(peers))


def gather_kernel(
    x, w, g, xall, b1, b2, kv, kvt, xg, gsend, grecv, sz, rz, sy, ry, sg, rg, lx, ll
):
    s, y, z = ring_place()
    p = 1 - y
    up = {"seq": y * NZ + lax.rem(z + 1, NZ)}
    down = {"seq": y * NZ + lax.rem(z + NZ - 1, NZ)}
    across = {"seq": p * NZ + z}
    load = pltpu.make_async_copy(x.at[0], xg.at[s], ll)
    load.start()
    greet([{"seq": lax.rem(s + d, NB)} for d in range(1, NB)])
    load.wait()

    def block(col, off):
        return col * NZ + lax.rem(z + off + NZ, NZ)

    def zmsg(flow, k, off, do_start):
        col = p if flow >= 4 else y
        part = 0 if flow < 2 else HALF
        rows = HALF
        if k == 3:
            rows = QUART
            part = part + (QUART if flow % 2 else 0)
        ref = xg.at[block(col, off), pl.ds(part, rows)]
        c = pltpu.make_async_remote_copy(
            src_ref=ref,
            dst_ref=ref,
            send_sem=sz.at[flow, k],
            recv_sem=rz.at[flow, k],
            device_id=down if flow % 2 else up,
            device_id_type=MESH,
        )
        if do_start:
            c.start()
        return c

    def ymsg(idx, col, do_start):
        off = 0 if idx == 8 else idx
        ref = xg.at[block(col, off), pl.ds(HALF if idx == 8 else 0, HALF)]
        c = pltpu.make_async_remote_copy(
            src_ref=ref,
            dst_ref=ref,
            send_sem=sy.at[idx],
            recv_sem=ry.at[idx],
            device_id=across,
            device_id_type=MESH,
        )
        if do_start:
            c.start()
        return c

    sent = []
    outs = []
    sent.append(ymsg(8, y, True))
    for flow in (2, 3, 0, 1):
        sent.append(zmsg(flow, 0, 0, True))
    sent.append(ymsg(0, y, True))

    def compute(b, n):
        xb = xg[b]
        at = pl.ds(pl.multiple_of(b * BLOCK, BLOCK), BLOCK)
        kvf = dot_t(xb, w[HD:, :])
        qt = dot_t(w[:HD, :], xb)
        zero = jnp.zeros((HD, BLOCK), F32)
        kv[at, :] = kvf.astype(BF)
        kvt[:, at] = kvf.T.astype(BF)
        b1[b, :HD, :] = jnp.concatenate([qt, zero], axis=1).astype(BF)
        b2[b, :BLOCK, :] = jnp.concatenate([qt, zero], axis=0).T.astype(BF)
        c = pltpu.make_async_copy(xg.at[b], xall.at[b], lx.at[n])
        c.start()
        outs.append(c)

    for c in range(NB // 2):
        t = g[0, :, c * BLOCK : (c + 1) * BLOCK].astype(F32).T.astype(BF)
        gsend[2 * c] = t[:HD]
        gsend[2 * c + 1] = t[HD:]

    def gmsg(d):
        to = lax.rem(s + d, NB)
        return pltpu.make_async_remote_copy(
            src_ref=gsend.at[to],
            dst_ref=grecv.at[s],
            send_sem=sg.at[d - 1],
            recv_sem=rg.at[d - 1],
            device_id={"seq": to},
            device_id_type=MESH,
        )

    compute(s, 0)
    ymsg(8, p, False).wait_recv()
    for flow in (4, 5):
        sent.append(zmsg(flow, 0, 0, True))
    for d in range(1, NB):
        c = gmsg(d)
        c.start()
        sent.append(c)
    grecv[s] = gsend[s]

    n = 1
    for k in range(4):
        for flow in (2, 3, 0, 1, 4, 5):
            off = (k + 1) if flow % 2 else -(k + 1)
            zmsg(flow, k, off, False).wait_recv()
            if k < 3:
                sent.append(zmsg(flow, k + 1, off, True))
            if flow < 2 and k < 3:
                sent.append(ymsg(off % NZ, y, True))
            if flow == 1 and k == 3:
                sent.append(ymsg(4, y, True))
        for off in [-(k + 1), k + 1][: 2 if k < 3 else 1]:
            compute(block(y, off), n)
            n += 1
        for off in [-k, k][: 2 if k > 0 else 1]:
            ymsg(off % NZ, p, False).wait_recv()
            compute(block(p, off), n)
            n += 1
    ymsg(4, p, False).wait_recv()
    compute(block(p, 4), n)
    for d in range(1, NB):
        frm = lax.rem(s + NB - d, NB)
        pltpu.make_async_remote_copy(
            src_ref=gsend.at[s],
            dst_ref=grecv.at[frm],
            send_sem=sg.at[d - 1],
            recv_sem=rg.at[d - 1],
            device_id={"seq": frm},
            device_id_type=MESH,
        ).wait_recv()

    def place(t, _):
        gt = grecv[t].astype(F32)
        zero = jnp.zeros((HD, BLOCK), F32)
        b1[t, HD:, :] = jnp.concatenate([zero, gt], axis=1).astype(BF)
        b2[t, BLOCK:, :] = jnp.concatenate([zero, gt], axis=0).T.astype(BF)
        return 0

    lax.fori_loop(0, NB, place, 0)
    for c in sent:
        c.wait_send()
    for c in outs:
        c.wait()


def gather(x, w, g):
    vm = pl.BlockSpec(memory_space=pltpu.VMEM)
    anyw = pl.BlockSpec(memory_space=pl.ANY)
    n = NB * BLOCK
    sem = pltpu.SemaphoreType.DMA
    return pl.pallas_call(
        gather_kernel,
        out_shape=(
            jax.ShapeDtypeStruct((NB, BLOCK, D), BF),
            jax.ShapeDtypeStruct((NB, BLOCK, 2 * BLOCK), BF),
            jax.ShapeDtypeStruct((NB, 2 * BLOCK, BLOCK), BF),
            jax.ShapeDtypeStruct((n, BLOCK), BF),
            jax.ShapeDtypeStruct((BLOCK, n), BF),
        ),
        in_specs=[anyw, vm, vm],
        out_specs=(anyw, vm, vm, vm, vm),
        scratch_shapes=[
            pltpu.VMEM((NB, BLOCK, D), BF),
            pltpu.VMEM((NB, HD, BLOCK), BF),
            pltpu.VMEM((NB, HD, BLOCK), BF),
            sem((6, 4)),
            sem((6, 4)),
            sem((9,)),
            sem((9,)),
            sem((NB - 1,)),
            sem((NB - 1,)),
            sem((NB,)),
            sem,
        ],
        compiler_params=pltpu.CompilerParams(
            collective_id=0, has_side_effects=True, vmem_limit_bytes=40 * 1024 * 1024
        ),
        name="gather_project",
    )(x, w, g)


def scatter_kernel(
    dproj, w, ot, xall,
    att, ng, wg,
    xv, zs, zr, ysb, yrb, arecv, dt, dwf, cs, cr, xs, xr, hs, hr, fs, fo, fsib,
    sz, rz, sy, ry, sa, ra, sc, rc, sx, rx, sh, rh, sf, rf, lx,
):
    s, y, z = ring_place()
    p = 1 - y
    up = {"seq": y * NZ + lax.rem(z + 1, NZ)}
    down = {"seq": y * NZ + lax.rem(z + NZ - 1, NZ)}
    across = {"seq": p * NZ + z}
    q = lax.axis_index("clus")
    cx = lax.div(q, NY * CORES)
    ch = lax.rem(lax.div(q, CORES), NY)
    cc = lax.rem(q, CORES)
    sib = {"clus": q + 1 - 2 * cc}

    def xpeer(d):
        return {"clus": lax.rem(cx + d, NX) * (NY * CORES) + ch * CORES + cc}

    def hpeer(d):
        return {"clus": cx * (NY * CORES) + lax.rem(ch + d, NY) * CORES + cc}

    load = pltpu.make_async_copy(xall, xv, lx)
    load.start()
    greet(
        [{"seq": lax.rem(s + d, NB)} for d in range(1, NB)]
        + [sib]
        + [xpeer(d) for d in range(1, NX)]
        + [hpeer(d) for d in range(1, NY)]
    )

    def block(col, off):
        return col * NZ + lax.rem(z + off + NZ, NZ)

    def part(col, off, first, rows):
        b = block(col, off)
        at = pl.ds(pl.multiple_of(b * BLOCK + first, QUART), rows)
        return jnp.dot(dproj[at, :], w[...], preferred_element_type=F32)

    sent = []

    def rcopy(src, dst, ss, rs, dev):
        return pltpu.make_async_remote_copy(
            src_ref=src, dst_ref=dst, send_sem=ss, recv_sem=rs,
            device_id=dev, device_id_type=MESH,
        )

    def span(flow, k):
        if k == 0:
            return pl.ds(QUART if flow % 2 else 0, QUART)
        return pl.ds(0, HALF)

    def zmsg(flow, k):
        at = span(flow, k)
        return rcopy(
            zs.at[flow, k, at], zr.at[flow, k, at], sz.at[flow, k], rz.at[flow, k],
            down if flow % 2 else up,
        )

    def ymsg(idx):
        return rcopy(ysb.at[idx], yrb.at[idx], sy.at[idx], ry.at[idx], across)

    def go(c):
        c.start()
        sent.append(c)

    def zstep(flow, k):
        col = p if flow >= 4 else y
        base = 0 if flow < 2 else HALF
        off = (4 - k) * (-1 if flow % 2 else 1)
        if k == 0:
            lo = QUART if flow % 2 else 0
            val = part(col, off, base + lo, QUART)
            if flow < 2:
                val = val + yrb[off % NZ, lo : lo + QUART, :].astype(F32)
            zs[flow, 0, lo : lo + QUART, :] = val.astype(BF)
        else:
            val = part(col, off, base, HALF)
            if flow < 2:
                val = val + yrb[off % NZ].astype(F32)
            zmsg(flow, k - 1).wait_recv()
            if k == 1:
                lo = QUART if flow % 2 else 0
                zs[flow, 1, QUART - lo : HALF - lo, :] = val[QUART - lo : HALF - lo].astype(BF)
                zs[flow, 1, lo : lo + QUART, :] = (
                    val[lo : lo + QUART] + zr[flow, 0, lo : lo + QUART, :].astype(F32)
                ).astype(BF)
            else:
                zs[flow, k] = (val + zr[flow, k - 1].astype(F32)).astype(BF)
        go(zmsg(flow, k))

    def ysend(off):
        ysb[off % NZ] = part(p, off, 0, HALF).astype(BF)
        go(ymsg(off % NZ))

    for flow in (2, 3):
        zstep(flow, 0)
    ysend(4)
    for flow in (4, 5):
        zstep(flow, 0)
    ysend(3)
    ysend(-3)
    for d in range(1, NB):
        to = lax.rem(s + d, NB)
        go(rcopy(ot.at[to], arecv.at[s], sa.at[d - 1], ra.at[d - 1], {"seq": to}))
    arecv[s] = ot[s]

    def turn(t, _):
        at = pl.ds(pl.multiple_of(t * BLOCK, BLOCK), BLOCK)
        v = jnp.concatenate([dproj[at, :].astype(F32), jnp.zeros((BLOCK, HD), F32)], axis=1)
        dt[:, at] = v.T[: 3 * HD].astype(BF)
        return 0

    def wstep(t, _):
        at = pl.ds(pl.multiple_of(t * 256, 256), 256)
        dwf[:, at] = jnp.dot(dt[...], xv[:, at], preferred_element_type=F32)
        return 0

    hrow = 3 * HD // CORES
    mine = pl.ds(pl.multiple_of(cc * hrow, QUART), hrow)
    other = pl.ds(pl.multiple_of((1 - cc) * hrow, QUART), hrow)
    wide = D // NX

    def stage0():
        lax.fori_loop(0, NB, turn, 0)
        load.wait()
        lax.fori_loop(0, D // 256, wstep, 0)
        cs[...] = dwf[other, :].astype(BF)
        go(rcopy(cs, cr, sc.at[0], rc.at[0], sib))

    def stage1():
        rcopy(cs, cr, sc.at[0], rc.at[0], sib).wait_recv()
        v = dwf[mine, :] + cr[...].astype(F32)
        for t in range(NX):
            xs[t] = v[:, t * wide : (t + 1) * wide].astype(BF)
        xr[cx] = xs[cx]
        for d in range(1, NX):
            go(rcopy(xs.at[lax.rem(cx + d, NX)], xr.at[cx], sx.at[d - 1], rx.at[d - 1], xpeer(d)))

    def stage2():
        for d in range(1, NX):
            frm = lax.rem(cx + NX - d, NX)
            rcopy(xs.at[cx], xr.at[frm], sx.at[d - 1], rx.at[d - 1], xpeer(d)).wait_recv()
        v = xr[0].astype(F32) + xr[1].astype(F32) + xr[2].astype(F32) + xr[3].astype(F32)
        hs[...] = v.astype(BF)
        hr[ch] = v.astype(BF)
        for d in range(1, NY):
            go(rcopy(hs, hr.at[ch], sh.at[d - 1], rh.at[d - 1], hpeer(d)))

    def stage3():
        for d in range(1, NY):
            frm = lax.rem(ch + NY - d, NY)
            rcopy(hs, hr.at[frm], sh.at[d - 1], rh.at[d - 1], hpeer(d)).wait_recv()
        v = hr[0].astype(F32) + hr[1].astype(F32) + hr[2].astype(F32) + hr[3].astype(F32)
        fs[...] = v.astype(BF)
        fo[cx] = v.astype(BF)
        for d in range(1, NX):
            go(rcopy(fs, fo.at[cx], sf.at[d - 1], rf.at[d - 1], xpeer(d)))

    def stage4():
        for d in range(1, NX):
            frm = lax.rem(cx + NX - d, NX)
            rcopy(fs, fo.at[frm], sf.at[d - 1], rf.at[d - 1], xpeer(d)).wait_recv()
        go(rcopy(fo, fsib, sc.at[1], rc.at[1], sib))

    def stage5():
        rcopy(fo, fsib, sc.at[1], rc.at[1], sib).wait_recv()
        for t in range(NX):
            at = pl.ds(t * wide, wide)
            wg[mine, at] = fo[t].astype(F32) * (1.0 / (NX * NY * CORES))
            wg[other, at] = fsib[t].astype(F32) * (1.0 / (NX * NY * CORES))

    def asteps(k):
        if k == 0:
            ymsg(4).wait_recv()
        else:
            ymsg((4 - k) % NZ).wait_recv()
            ymsg((k - 4) % NZ).wait_recv()
        zstep(0, k)
        zstep(1, k)

    stage0()
    asteps(0)
    for flow in (2, 3, 4, 5):
        zstep(flow, 1)
    ysend(2)
    ysend(-2)
    asteps(1)
    stage1()
    for flow in (2, 3, 4, 5):
        zstep(flow, 2)
    ysend(1)
    ysend(-1)
    asteps(2)
    stage2()
    for flow in (4, 5, 2, 3):
        zstep(flow, 3)
    ysend(0)
    asteps(3)
    stage3()

    def total(flow, col, base):
        val = part(col, 0, base, HALF)
        for f in (flow, flow + 1):
            zmsg(f, 3).wait_recv()
            val = val + zr[f, 3].astype(F32)
        return val

    ysb[8] = total(4, p, HALF).astype(BF)
    go(ymsg(8))
    stage4()
    own_b = total(2, y, HALF)
    ymsg(0).wait_recv()
    ng[0, :HALF, :] = (total(0, y, 0) + yrb[0].astype(F32)).astype(BF)
    for d in range(1, NB):
        frm = lax.rem(s + NB - d, NB)
        rcopy(ot.at[s], arecv.at[frm], sa.at[d - 1], ra.at[d - 1], {"seq": frm}).wait_recv()
    for c in range(NB // 2):
        t = jnp.concatenate([arecv[2 * c], arecv[2 * c + 1]], axis=0).astype(F32)
        att[0, :, c * BLOCK : (c + 1) * BLOCK] = t.T.astype(BF)
    stage5()
    ymsg(8).wait_recv()
    ng[0, HALF:, :] = (own_b + yrb[8].astype(F32)).astype(BF)
    for c in sent:
        c.wait_send()


def scatter(dproj, w, ot, xall):
    vm = pl.BlockSpec(memory_space=pltpu.VMEM)
    anyw = pl.BlockSpec(memory_space=pl.ANY)
    n = NB * BLOCK
    sem = pltpu.SemaphoreType.DMA
    vmem = pltpu.VMEM
    hrow = 3 * HD // CORES
    wide = D // NX
    return pl.pallas_call(
        scatter_kernel,
        out_shape=(
            jax.ShapeDtypeStruct((1, BLOCK, D), BF),
            jax.ShapeDtypeStruct((1, BLOCK, D), BF),
            jax.ShapeDtypeStruct((3 * HD, D), F32),
        ),
        in_specs=[vm, vm, vm, anyw],
        out_specs=(vm, vm, vm),
        scratch_shapes=[
            vmem((n, D), BF),
            vmem((6, 4, HALF, D), BF),
            vmem((6, 4, HALF, D), BF),
            vmem((9, HALF, D), BF),
            vmem((9, HALF, D), BF),
            vmem((NB, HD, BLOCK), BF),
            vmem((3 * HD, n), BF),
            vmem((3 * HD, D), F32),
            vmem((hrow, D), BF),
            vmem((hrow, D), BF),
            vmem((NX, hrow, wide), BF),
            vmem((NX, hrow, wide), BF),
            vmem((hrow, wide), BF),
            vmem((NY, hrow, wide), BF),
            vmem((hrow, wide), BF),
            vmem((NX, hrow, wide), BF),
            vmem((NX, hrow, wide), BF),
            sem((6, 4)),
            sem((6, 4)),
            sem((9,)),
            sem((9,)),
            sem((NB - 1,)),
            sem((NB - 1,)),
            sem((2,)),
            sem((2,)),
            sem((NX - 1,)),
            sem((NX - 1,)),
            sem((NY - 1,)),
            sem((NY - 1,)),
            sem((NX - 1,)),
            sem((NX - 1,)),
            sem,
        ],
        compiler_params=pltpu.CompilerParams(
            collective_id=1, has_side_effects=True, vmem_limit_bytes=60 * 1024 * 1024
        ),
        name="scatter_reduce",
    )(dproj, w, ot, xall)


def local(node_feats, qkv_weight, block_pairs, grad_out):
    xall, b1, b2, kv, kvt = gather(node_feats, qkv_weight, grad_out)
    ot, dproj = attention(block_pairs.reshape(-1), b1, b2, kv, kvt)
    return scatter(dproj, qkv_weight, ot, xall.reshape(NB * BLOCK, D))


def solution(mesh):
    return jax.shard_map(
        local,
        mesh=mesh,
        in_specs=(
            P("clus", "seq", None),
            P("seq", None),
            P("clus", None, None),
            P("clus", "seq", None),
        ),
        out_specs=(P("clus", "seq", None), P("clus", "seq", None), P("seq", None)),
        check_vma=False,
    )
```

time: 564 us -> 147 us (0.26)
  the two profiles are of different devices: /device:TPU:6 before, /device:TPU:1 now
where the time goes in v1:
time: 147 us
  Pallas kernels  133 us (90%)
  local copies, waits for them, and re-layouts  12.8 us (9%)
    pallas_call x1, Pallas kernels, gather(): pl.pallas_call(gather_kernel, out_shape=(jax.ShapeDtypeStruct((NB, BLOCK,...  52.5 us
    pallas_call x1, Pallas kernels, scatter(): pl.pallas_call(scatter_kernel, out_shape=(jax.ShapeDtypeStruct((1, BLOCK,...  50.8 us
    pallas_call x1, Pallas kernels, attention(): pl.pallas_call(attn_kernel, out_shape=(jax.ShapeDtypeStruct((NB, HD, BLOC...  29.7 us
    unnamed x16, local copies, waits for them, and re-layouts  12.7 us

profile of v1, /device:TPU:1, one launch (start us, length us, event | category | flops | bytes accessed | tf_op | source)
XLA Modules:
  0.0 146.6 jit_solution(8012494302593761923)
XLA Ops:
  0.6 0.8 copy.7
  1.4 0.1 reshape.12.pairs
  1.6 0.0 copy-start.1
  1.6 1.0 copy-done.1
  2.6 0.0 copy-start.3
  2.6 0.9 copy-done.3
  3.5 0.0 copy-start.4
  3.5 0.9 copy-done.4
  4.5 52.5 %gather_project.1 = (bf16[16,128,1024]{2,1,0:T(8,128)(2,1)S(1)}, bf16[16,128,256]{2,1,0:T(8,128)(2,1)S(1)}, bf16[16,256,128]{2,1,0:T(8,128)(2,1)S(1)}, bf16[2048...) custom-call(bf16[1,128,1024]{2,1,0:T(8,128)(2,1)S(1)} %copy-done.3, bf16[192,1024]{1,0:T(8,128)(2,1)S(1)} %copy-done.1, ...), custom_call_target="tpu_custom_call" | custom-call | tf_op jit(solution)/shard_map/gather_project/pallas_call | solution.py:321
  57.0 0.0 copy-start
  57.0 1.9 %copy-done = bf16[16,128,1024]{2,1,0:T(8,128)(2,1)} copy-done((bf16[16,128,1024]{2,1,0:T(8,128)(2,1)}, bf16[16,128,1024]{2,1,0:T(8,128)(2,1)S(1)}, u32[]{:S(2)}) %copy-start) | copy-done | bytes 4194328
  58.9 29.7 %attention.1 = (bf16[16,64,128]{2,1,0:T(8,128)(2,1)S(1)}, bf16[2048,192]{1,0:T(8,128)(2,1)S(1)}) custom-call(s32[256]{0:T(256)S(1)} %reshape.12.pairs, bf16[16,128,256]{2,1,0:T(8,128)(2,1)S(1)} %get-tuple-element.10.b1, bf16[16,256,128]{2,1,0:T(8,128)(2,1)S(1)} %get-tuple-element.11.b2, bf16[2048,128]{1,0:T(8,128)(2,1)S(1)} %get-tuple-element.12.kv, ...), custom_call_target="tpu_custom_call" | custom-call | tf_op jit(solution)/shard_map/attention/pallas_call | solution.py:123
  88.6 0.0 copy-start.2
  88.7 1.0 copy-done.2
  89.6 0.0 copy-start.5
  89.6 0.7 copy-done.5
  90.3 50.8 %scatter_reduce.1 = (bf16[1,128,1024]{2,1,0:T(8,128)(2,1)}, bf16[1,128,1024]{2,1,0:T(8,128)(2,1)}, f32[192,1024]{1,0:T(8,128)}) custom-call(bf16[2048,192]{1,0:T(8,128)(2,1)} %copy-done.2, bf16[192,1024]{1,0:T(8,128)(2,1)} %w.3, bf16[16,64,128]{2,1,0:T(8,128)(2,1)} %copy-done.5, bf16[2048,1024]{1,0:T(8,128)(2,1)} %bitcast.1), custom_call_target="tpu_custom_call" | custom-call | tf_op jit(solution)/shard_map/scatter_reduce/pallas_call | solution.py:588
  141.1 1.7 %copy.11 = bf16[1,128,1024]{2,1,0:T(8,128)(2,1)} copy(bf16[1,128,1024]{2,1,0:T(8,128)(2,1)} %get-tuple-element.20) | data formatting | bytes 524288
  142.8 1.7 %copy.12 = bf16[1,128,1024]{2,1,0:T(8,128)(2,1)} copy(bf16[1,128,1024]{2,1,0:T(8,128)(2,1)} %get-tuple-element.21) | data formatting | bytes 524288
  144.5 2.1 %copy.13 = f32[192,1024]{1,0:T(8,128)} copy(f32[192,1024]{1,0:T(8,128)} %get-tuple-element.22) | data formatting | bytes 1572864
Async XLA Ops:
  1.6 1.0 copy-start.1
  2.6 0.9 copy-start.3
  3.5 0.9 copy-start.4
  57.0 1.9 %copy-start = (bf16[16,128,1024]{2,1,0:T(8,128)(2,1)}, bf16[16,128,1024]{2,1,0:T(8,128)(2,1)S(1)}, u32[]{:S(2)}) copy-start(bf16[16,128,1024]{2,1,0:T(8,128)(2,1)S(1)} %get-tuple-element.16) | copy-start | bytes 12582916
  88.6 1.0 copy-start.2
  89.6 0.7 copy-start.5

commit v2 on v1

--- a/solution.py
+++ b/solution.py
@@ -1,3 +1,5 @@
+import math
+
 import jax
 import jax.numpy as jnp
 from jax import lax
@@ -13,113 +15,109 @@
 CH = 4
 ROWS = CH * BLOCK
 PAD = -1e30
-
-
-def attn_kernel(pairs, b1, b2, kv, kvt, ot, dproj, cols, cnt, s_scr, d_scr, acc):
-    npairs = pairs.shape[0] // 2
-
-    def clear(t, _):
-        cols[t] = 0
+COUNT = 16
+ROWID = 17
+SCALE = 0.125 * math.log2(math.e)
+
+
+def attn_kernel(lst, b1, b2, kv, kvt, ot, dproj, s_scr, d_scr, acc):
+    acc[...] = jnp.zeros_like(acc)
+
+    def at_block(j):
+        return pl.ds(pl.multiple_of(j * BLOCK, BLOCK), BLOCK)
+
+    def at_chunk(c):
+        return pl.ds(pl.multiple_of(c * ROWS, ROWS), ROWS)
+
+    def chunks(r):
+        return lax.div(lst[r, COUNT] + (CH - 1), CH)
+
+    def scores(r, c, buf, w1, m):
+        n = lst[r, COUNT]
+        lhs = jnp.concatenate([kv[at_block(lst[r, c * CH + t]), :] for t in range(CH)], axis=0)
+        sd = jnp.dot(lhs, w1, preferred_element_type=F32)
+        s = jnp.concatenate(
+            [
+                sd[t * BLOCK : (t + 1) * BLOCK, :BLOCK]
+                + jnp.where(c * CH + t < n, 0.0, PAD).astype(F32)
+                for t in range(CH)
+            ],
+            axis=0,
+        )
+        s_scr[buf, at_chunk(c), :] = s
+        d_scr[buf, at_chunk(c), :] = sd[:, BLOCK:]
+        return jnp.maximum(m, jnp.max(s.reshape(ROWS // 8, 8, BLOCK), axis=0))
+
+    def weigh(r, buf, m):
+        m = jnp.max(m, axis=0, keepdims=True)
+
+        def step(c, carry):
+            l, d = carry
+            e = jnp.exp2((s_scr[buf, at_chunk(c), :] - m) * SCALE)
+            s_scr[buf, at_chunk(c), :] = e
+            l = l + jnp.sum(e.reshape(ROWS // 8, 8, BLOCK), axis=0)
+            ed = e * d_scr[buf, at_chunk(c), :]
+            d = d + jnp.sum(ed.reshape(ROWS // 8, 8, BLOCK), axis=0)
+            return l, d
+
+        zero = jnp.zeros((8, BLOCK), F32)
+        l, d = lax.fori_loop(0, chunks(r), step, (zero, zero))
+        linv = 1.0 / jnp.sum(l, axis=0, keepdims=True)
+        return linv, jnp.sum(d, axis=0, keepdims=True) * linv
+
+    def gradients(r, c, buf, w2, linv, delta, oq):
+        e = s_scr[buf, at_chunk(c), :]
+        p = e * linv
+        ds = p * ((d_scr[buf, at_chunk(c), :] - delta) * 0.125)
+        cat = jnp.concatenate([ds.astype(BF), p.astype(BF)], axis=1)
+        cols = [lst[r, c * CH + t] for t in range(CH)]
+        lhs = jnp.concatenate([kvt[:, at_block(j)] for j in cols], axis=1)
+        oq = oq + jnp.dot(lhs, cat, preferred_element_type=F32)
+        g = jnp.dot(cat, w2, preferred_element_type=F32)
+        for t in range(CH):
+            acc[at_block(cols[t]), :] += g[t * BLOCK : (t + 1) * BLOCK]
+        return oq
+
+    low = jnp.full((8, BLOCK), PAD, F32)
+    first = b1[lst[0, ROWID]]
+    m0 = lax.fori_loop(0, chunks(0), lambda c, m: scores(0, c, 0, first, m), low)
+    linv0, delta0 = weigh(0, 0, m0)
+
+    def row(r, carry):
+        linv, delta = carry
+        i = lst[r, ROWID]
+        buf = lax.rem(r, 2)
+        nxt = jnp.minimum(r + 1, NB - 1)
+        w1 = b1[lst[nxt, ROWID]]
+        w2 = b2[i]
+
+        def both(c, state):
+            oq, m = state
+            m = scores(nxt, c, 1 - buf, w1, m)
+            oq = gradients(r, c, buf, w2, linv, delta, oq)
+            return oq, m
+
+        oq, m = lax.fori_loop(
+            0, chunks(r), both, (jnp.zeros((BLOCK, 2 * BLOCK), F32), low)
+        )
+        ot[i] = oq[HD:, BLOCK:].astype(BF)
+        dproj[at_block(i), 0:BLOCK] = oq[:, :BLOCK].T.astype(BF)
+        return weigh(nxt, 1 - buf, m)
+
+    lax.fori_loop(0, NB, row, (linv0, delta0))
+
+    def fin(i, _):
+        a = acc[at_block(i), :].astype(BF)
+        q = dproj[at_block(i), 0:BLOCK]
+        dproj[at_block(i), :] = jnp.concatenate([q[:, :HD], a], axis=1)
         return 0
 
-    lax.fori_loop(0, NB * NB, clear, 0)
-
-    def clear_cnt(t, _):
-        cnt[t] = 0
-        return 0
-
-    lax.fori_loop(0, NB, clear_cnt, 0)
-
-    def put(t, _):
-        r = pairs[2 * t]
-        n = cnt[r]
-        cols[r * NB + n] = pairs[2 * t + 1]
-        cnt[r] = n + 1
-        return 0
-
-    lax.fori_loop(0, npairs, put, 0)
-    acc[...] = jnp.zeros_like(acc)
-
-    def row(i, _):
-        n = cnt[i]
-        nch = (n + CH - 1) // CH
-        w1 = b1[i]
-        w2 = b2[i]
-
-        def pass1(c, m):
-            for t in range(CH):
-                slot = c * CH + t
-                j = cols[i * NB + slot]
-                blk = kv[pl.ds(pl.multiple_of(j * BLOCK, BLOCK), BLOCK), :]
-                sd = jnp.dot(blk, w1, preferred_element_type=F32)
-                bias = jnp.where(slot < n, 0.0, PAD).astype(F32)
-                s = sd[:, :BLOCK] + bias
-                at = pl.ds(pl.multiple_of(slot * BLOCK, BLOCK), BLOCK)
-                s_scr[at, :] = s
-                d_scr[at, :] = sd[:, BLOCK:]
-                m = jnp.maximum(m, jnp.max(s.reshape(16, 8, BLOCK), axis=0))
-            return m
-
-        m = lax.fori_loop(0, nch, pass1, jnp.full((8, BLOCK), PAD, F32))
-        m = jnp.max(m, axis=0, keepdims=True)
-
-        def pass2(c, carry):
-            l, d = carry
-            at = pl.ds(pl.multiple_of(c * ROWS, ROWS), ROWS)
-            e = jnp.exp((s_scr[at, :] - m) * 0.125)
-            s_scr[at, :] = e
-            l = l + jnp.sum(e.reshape(ROWS // 8, 8, BLOCK), axis=0)
-            d = d + jnp.sum((e * d_scr[at, :]).reshape(ROWS // 8, 8, BLOCK), axis=0)
-            return l, d
-
-        zero = jnp.zeros((8, BLOCK), F32)
-        l, d = lax.fori_loop(0, nch, pass2, (zero, zero))
-        linv = 1.0 / jnp.sum(l, axis=0, keepdims=True)
-        delta = jnp.sum(d, axis=0, keepdims=True) * linv
-        lscale = linv * 0.125
-
-        def pass3(c, oq):
-            at = pl.ds(pl.multiple_of(c * ROWS, ROWS), ROWS)
-            e = s_scr[at, :]
-            p = (e * linv).astype(BF)
-            ds = (e * lscale * (d_scr[at, :] - delta)).astype(BF)
-            cat = jnp.concatenate([ds, p], axis=1)
-            lhs = jnp.concatenate(
-                [
-                    kvt[:, pl.ds(pl.multiple_of(cols[i * NB + c * CH + t] * BLOCK, BLOCK), BLOCK)]
-                    for t in range(CH)
-                ],
-                axis=1,
-            )
-            oq = oq + jnp.dot(lhs, cat, preferred_element_type=F32)
-            g = jnp.dot(cat, w2, preferred_element_type=F32)
-            for t in range(CH):
-                j = cols[i * NB + c * CH + t]
-                aj = pl.ds(pl.multiple_of(j * BLOCK, BLOCK), BLOCK)
-                acc[aj, :] += g[t * BLOCK : (t + 1) * BLOCK]
-            return oq
-
-        oq = lax.fori_loop(0, nch, pass3, jnp.zeros((BLOCK, 2 * BLOCK), F32))
-        here = pl.ds(pl.multiple_of(i * BLOCK, BLOCK), BLOCK)
-        ot[i] = oq[HD:, BLOCK:].astype(BF)
-        dproj[here, 0:BLOCK] = oq[:, :BLOCK].T.astype(BF)
-        return 0
-
-    lax.fori_loop(0, NB, row, 0)
-
-    def fin(i, _):
-        here = pl.ds(pl.multiple_of(i * BLOCK, BLOCK), BLOCK)
-        a = acc[here, :].astype(BF)
-        q = dproj[here, 0:BLOCK]
-        dproj[here, :] = jnp.concatenate([q[:, :HD], a], axis=1)
-        return 0
-
-    lax.fori_loop(0, NB, fin, 0)
-
-
-def attention(pairs, b1, b2, kv, kvt):
+    lax.fori_loop(0, NB, fin, 0, unroll=4)
+
+
+def attention(lst, b1, b2, kv, kvt):
     vm = pl.BlockSpec(memory_space=pltpu.VMEM)
-    n = kv.shape[0]
+    n = NB * BLOCK
     return pl.pallas_call(
         attn_kernel,
         out_shape=(
@@ -129,15 +127,13 @@
         in_specs=[pl.BlockSpec(memory_space=pltpu.SMEM), vm, vm, vm, vm],
         out_specs=(vm, vm),
         scratch_shapes=[
-            pltpu.SMEM((NB * NB,), jnp.int32),
-            pltpu.SMEM((NB,), jnp.int32),
-            pltpu.VMEM((n, BLOCK), F32),
-            pltpu.VMEM((n, BLOCK), F32),
+            pltpu.VMEM((2, n, BLOCK), F32),
+            pltpu.VMEM((2, n, BLOCK), F32),
             pltpu.VMEM((n, BLOCK), F32),
         ],
-        compiler_params=pltpu.CompilerParams(vmem_limit_bytes=40 * 1024 * 1024),
+        compiler_params=pltpu.CompilerParams(vmem_limit_bytes=12 * 1024 * 1024),
         name="attention",
-    )(pairs, b1, b2, kv, kvt)
+    )(lst, b1, b2, kv, kvt)
 
 MESH = pl.DeviceIdType.MESH
 HD = 64
@@ -170,16 +166,56 @@
     pl.semaphore_wait(barrier, len(peers))
 
 
+RA = 80
+SPLIT = {0: (0, 48), 1: (48, 32), 2: (80, 16), 3: (96, 32)}
+
+
+def row_lists(pairs):
+    one = jnp.float32(1)
+    sub = lax.broadcasted_iota(jnp.int32, (BLOCK, BLOCK), 0)
+    lane = lax.broadcasted_iota(jnp.int32, (BLOCK, BLOCK), 1)
+    sub_nb, lane_nb = sub[:NB], lane[:NB]
+    row_hot = jnp.where(sub == pairs[0:1, :], one, 0.0).astype(BF)
+    col_hot = jnp.where(sub == pairs[1:2, :], one, 0.0).astype(BF)
+    allowed = dot_t(row_hot[:NB], col_hot)
+    n_col = jnp.sum(allowed, axis=1, keepdims=True)
+    n_row = dot_t(jnp.ones((NB, BLOCK), BF), row_hot)[0:1]
+    before = jnp.where(sub < lane, one, 0.0).astype(BF)
+    pos = jnp.dot(allowed.astype(BF), before, preferred_element_type=F32)
+    lists = jnp.zeros((NB, BLOCK), F32)
+    lane_f = lane_nb.astype(F32)
+    for t in range(NB):
+        hit = jnp.where(pos == t, allowed, 0.0)
+        col = jnp.sum(hit * lane_f, axis=1, keepdims=True)
+        lists = jnp.where(lane_nb == t, col, lists)
+    lists = jnp.where(lane_nb == NB, n_col, lists)
+    lists = jnp.where(lane_nb == NB + 1, sub_nb.astype(F32), lists)
+    ahead = jnp.logical_or(n_col > n_row, jnp.logical_and(n_col == n_row, sub_nb < lane_nb))
+    rank = jnp.sum(jnp.where(ahead, one, 0.0), axis=0, keepdims=True)
+    move = jnp.where(jnp.logical_and(sub_nb.astype(F32) == rank, lane_nb < NB), one, 0.0)
+    full = jnp.concatenate([lists, jnp.zeros((BLOCK - NB, BLOCK), F32)], axis=0)
+    out = jnp.dot(move.astype(BF), full.astype(BF), preferred_element_type=F32)
+    return (out + 0.5).astype(jnp.int32)
+
+
 def gather_kernel(
-    x, w, g, xall, b1, b2, kv, kvt, xg, gsend, grecv, sz, rz, sy, ry, sg, rg, lx, ll
+    x, w_hbm, g_hbm, pairs_hbm,
+    xall, b1, b2, kv, kvt, lst,
+    w, g, pairs, xg, gsend, grecv, sz, rz, sy, ry, sg, rg, lx, ll,
 ):
     s, y, z = ring_place()
     p = 1 - y
     up = {"seq": y * NZ + lax.rem(z + 1, NZ)}
     down = {"seq": y * NZ + lax.rem(z + NZ - 1, NZ)}
     across = {"seq": p * NZ + z}
-    load = pltpu.make_async_copy(x.at[0], xg.at[s], ll)
+    load = pltpu.make_async_copy(x.at[0], xg.at[s], ll.at[0])
+    load_g = pltpu.make_async_copy(g_hbm.at[0], g, ll.at[1])
+    load_w = pltpu.make_async_copy(w_hbm, w, ll.at[2])
+    load_p = pltpu.make_async_copy(pairs_hbm, pairs, ll.at[3])
     load.start()
+    load_g.start()
+    load_w.start()
+    load_p.start()
     greet([{"seq": lax.rem(s + d, NB)} for d in range(1, NB)])
     load.wait()
 
@@ -188,12 +224,10 @@
 
     def zmsg(flow, k, off, do_start):
         col = p if flow >= 4 else y
-        part = 0 if flow < 2 else HALF
-        rows = HALF
+        first, rows = (0, RA) if flow < 2 else (RA, BLOCK - RA)
         if k == 3:
-            rows = QUART
-            part = part + (QUART if flow % 2 else 0)
-        ref = xg.at[block(col, off), pl.ds(part, rows)]
+            first, rows = SPLIT[flow - 2 if flow >= 4 else flow]
+        ref = xg.at[block(col, off), pl.ds(first, rows)]
         c = pltpu.make_async_remote_copy(
             src_ref=ref,
             dst_ref=ref,
@@ -208,7 +242,7 @@
 
     def ymsg(idx, col, do_start):
         off = 0 if idx == 8 else idx
-        ref = xg.at[block(col, off), pl.ds(HALF if idx == 8 else 0, HALF)]
+        ref = xg.at[block(col, off), pl.ds(RA, BLOCK - RA) if idx == 8 else pl.ds(0, RA)]
         c = pltpu.make_async_remote_copy(
             src_ref=ref,
             dst_ref=ref,
@@ -224,7 +258,7 @@
     sent = []
     outs = []
     sent.append(ymsg(8, y, True))
-    for flow in (2, 3, 0, 1):
+    for flow in (0, 1, 2, 3):
         sent.append(zmsg(flow, 0, 0, True))
     sent.append(ymsg(0, y, True))
 
@@ -242,8 +276,9 @@
         c.start()
         outs.append(c)
 
+    load_g.wait()
     for c in range(NB // 2):
-        t = g[0, :, c * BLOCK : (c + 1) * BLOCK].astype(F32).T.astype(BF)
+        t = g[:, c * BLOCK : (c + 1) * BLOCK].astype(F32).T.astype(BF)
         gsend[2 * c] = t[:HD]
         gsend[2 * c + 1] = t[HD:]
 
@@ -258,6 +293,7 @@
             device_id_type=MESH,
         )
 
+    load_w.wait()
     compute(s, 0)
     ymsg(8, p, False).wait_recv()
     for flow in (4, 5):
@@ -267,10 +303,32 @@
         c.start()
         sent.append(c)
     grecv[s] = gsend[s]
+    load_p.wait()
+    lst[...] = row_lists(pairs[...])
+
+    def place(t, _):
+        gt = grecv[t].astype(F32)
+        zero = jnp.zeros((HD, BLOCK), F32)
+        b1[t, HD:, :] = jnp.concatenate([zero, gt], axis=1).astype(BF)
+        b2[t, BLOCK:, :] = jnp.concatenate([zero, gt], axis=0).T.astype(BF)
+        return 0
+
+    def place_all():
+        for d in range(1, NB):
+            frm = lax.rem(s + NB - d, NB)
+            pltpu.make_async_remote_copy(
+                src_ref=gsend.at[s],
+                dst_ref=grecv.at[frm],
+                send_sem=sg.at[d - 1],
+                recv_sem=rg.at[d - 1],
+                device_id={"seq": frm},
+                device_id_type=MESH,
+            ).wait_recv()
+        lax.fori_loop(0, NB, place, 0)
 
     n = 1
     for k in range(4):
-        for flow in (2, 3, 0, 1, 4, 5):
+        for flow in (0, 1, 2, 3, 4, 5):
             off = (k + 1) if flow % 2 else -(k + 1)
             zmsg(flow, k, off, False).wait_recv()
             if k < 3:
@@ -286,36 +344,23 @@
             ymsg(off % NZ, p, False).wait_recv()
             compute(block(p, off), n)
             n += 1
+        if k == 2:
+            place_all()
+    for c in outs:
+        c.wait()
+    outs.clear()
     ymsg(4, p, False).wait_recv()
     compute(block(p, 4), n)
-    for d in range(1, NB):
-        frm = lax.rem(s + NB - d, NB)
-        pltpu.make_async_remote_copy(
-            src_ref=gsend.at[s],
-            dst_ref=grecv.at[frm],
-            send_sem=sg.at[d - 1],
-            recv_sem=rg.at[d - 1],
-            device_id={"seq": frm},
-            device_id_type=MESH,
-        ).wait_recv()
-
-    def place(t, _):
-        gt = grecv[t].astype(F32)
-        zero = jnp.zeros((HD, BLOCK), F32)
-        b1[t, HD:, :] = jnp.concatenate([zero, gt], axis=1).astype(BF)
-        b2[t, BLOCK:, :] = jnp.concatenate([zero, gt], axis=0).T.astype(BF)
-        return 0
-
-    lax.fori_loop(0, NB, place, 0)
     for c in sent:
         c.wait_send()
     for c in outs:
         c.wait()
 
 
-def gather(x, w, g):
+def gather(x, w, g, pairs):
     vm = pl.BlockSpec(memory_space=pltpu.VMEM)
     anyw = pl.BlockSpec(memory_space=pl.ANY)
+    hbm = pl.BlockSpec(memory_space=pltpu.HBM)
     n = NB * BLOCK
     sem = pltpu.SemaphoreType.DMA
     return pl.pallas_call(
@@ -326,10 +371,14 @@
             jax.ShapeDtypeStruct((NB, 2 * BLOCK, BLOCK), BF),
             jax.ShapeDtypeStruct((n, BLOCK), BF),
             jax.ShapeDtypeStruct((BLOCK, n), BF),
+            jax.ShapeDtypeStruct((NB, BLOCK), jnp.int32),
         ),
-        in_specs=[anyw, vm, vm],
-        out_specs=(anyw, vm, vm, vm, vm),
+        in_specs=[hbm, hbm, hbm, hbm],
+        out_specs=(anyw, vm, vm, vm, vm, vm),
         scratch_shapes=[
+            pltpu.VMEM((3 * HD, D), BF),
+            pltpu.VMEM((BLOCK, D), BF),
+            pltpu.VMEM((2, BLOCK), jnp.int32),
             pltpu.VMEM((NB, BLOCK, D), BF),
             pltpu.VMEM((NB, HD, BLOCK), BF),
             pltpu.VMEM((NB, HD, BLOCK), BF),
@@ -340,19 +389,19 @@
             sem((NB - 1,)),
             sem((NB - 1,)),
             sem((NB,)),
-            sem,
+            sem((4,)),
         ],
         compiler_params=pltpu.CompilerParams(
-            collective_id=0, has_side_effects=True, vmem_limit_bytes=40 * 1024 * 1024
+            collective_id=0, has_side_effects=True, vmem_limit_bytes=20 * 1024 * 1024
         ),
         name="gather_project",
-    )(x, w, g)
+    )(x, w, g, pairs)
 
 
 def scatter_kernel(
-    dproj, w, ot, xall,
+    dproj, w_hbm, ot, xv,
     att, ng, wg,
-    xv, zs, zr, ysb, yrb, arecv, dt, dwf, cs, cr, xs, xr, hs, hr, fs, fo, fsib,
+    w, zs, zr, ysb, yrb, arecv, dt, dwf, cs, cr, xs, xr, hs, hr, fs, fo, fsib,
     sz, rz, sy, ry, sa, ra, sc, rc, sx, rx, sh, rh, sf, rf, lx,
 ):
     s, y, z = ring_place()
@@ -372,7 +421,7 @@
     def hpeer(d):
         return {"clus": cx * (NY * CORES) + lax.rem(ch + d, NY) * CORES + cc}
 
-    load = pltpu.make_async_copy(xall, xv, lx)
+    load = pltpu.make_async_copy(w_hbm, w, lx)
     load.start()
     greet(
         [{"seq": lax.rem(s + d, NB)} for d in range(1, NB)]
@@ -445,10 +494,11 @@
         ysb[off % NZ] = part(p, off, 0, HALF).astype(BF)
         go(ymsg(off % NZ))
 
-    for flow in (2, 3):
+    load.wait()
+    for flow in (4, 5):
         zstep(flow, 0)
     ysend(4)
-    for flow in (4, 5):
+    for flow in (2, 3):
         zstep(flow, 0)
     ysend(3)
     ysend(-3)
@@ -473,10 +523,12 @@
     other = pl.ds(pl.multiple_of((1 - cc) * hrow, QUART), hrow)
     wide = D // NX
 
-    def stage0():
+    def stage0a():
         lax.fori_loop(0, NB, turn, 0)
-        load.wait()
-        lax.fori_loop(0, D // 256, wstep, 0)
+        lax.fori_loop(0, 2, wstep, 0)
+
+    def stage0b():
+        lax.fori_loop(2, D // 256, wstep, 0)
         cs[...] = dwf[other, :].astype(BF)
         go(rcopy(cs, cr, sc.at[0], rc.at[0], sib))
 
@@ -531,26 +583,6 @@
         zstep(0, k)
         zstep(1, k)
 
-    stage0()
-    asteps(0)
-    for flow in (2, 3, 4, 5):
-        zstep(flow, 1)
-    ysend(2)
-    ysend(-2)
-    asteps(1)
-    stage1()
-    for flow in (2, 3, 4, 5):
-        zstep(flow, 2)
-    ysend(1)
-    ysend(-1)
-    asteps(2)
-    stage2()
-    for flow in (4, 5, 2, 3):
-        zstep(flow, 3)
-    ysend(0)
-    asteps(3)
-    stage3()
-
     def total(flow, col, base):
         val = part(col, 0, base, HALF)
         for f in (flow, flow + 1):
@@ -558,10 +590,30 @@
             val = val + zr[f, 3].astype(F32)
         return val
 
+    asteps(0)
+    for flow in (4, 5, 2, 3):
+        zstep(flow, 1)
+    ysend(2)
+    ysend(-2)
+    stage0a()
+    asteps(1)
+    for flow in (4, 5, 2, 3):
+        zstep(flow, 2)
+    ysend(1)
+    ysend(-1)
+    stage0b()
+    asteps(2)
+    stage1()
+    for flow in (4, 5, 2, 3):
+        zstep(flow, 3)
+    ysend(0)
+    stage2()
+    asteps(3)
     ysb[8] = total(4, p, HALF).astype(BF)
     go(ymsg(8))
+    stage3()
+    own_b = total(2, y, HALF)
     stage4()
-    own_b = total(2, y, HALF)
     ymsg(0).wait_recv()
     ng[0, :HALF, :] = (total(0, y, 0) + yrb[0].astype(F32)).astype(BF)
     for d in range(1, NB):
@@ -579,7 +631,7 @@
 
 def scatter(dproj, w, ot, xall):
     vm = pl.BlockSpec(memory_space=pltpu.VMEM)
-    anyw = pl.BlockSpec(memory_space=pl.ANY)
+    hbm = pl.BlockSpec(memory_space=pltpu.HBM)
     n = NB * BLOCK
     sem = pltpu.SemaphoreType.DMA
     vmem = pltpu.VMEM
@@ -592,10 +644,10 @@
             jax.ShapeDtypeStruct((1, BLOCK, D), BF),
             jax.ShapeDtypeStruct((3 * HD, D), F32),
         ),
-        in_specs=[vm, vm, vm, anyw],
+        in_specs=[vm, hbm, vm, vm],
         out_specs=(vm, vm, vm),
         scratch_shapes=[
-            vmem((n, D), BF),
+            vmem((3 * HD, D), BF),
             vmem((6, 4, HALF, D), BF),
             vmem((6, 4, HALF, D), BF),
             vmem((9, HALF, D), BF),
@@ -629,16 +681,43 @@
             sem,
         ],
         compiler_params=pltpu.CompilerParams(
-            collective_id=1, has_side_effects=True, vmem_limit_bytes=60 * 1024 * 1024
+            collective_id=1, has_side_effects=True, vmem_limit_bytes=22 * 1024 * 1024
         ),
         name="scatter_reduce",
     )(dproj, w, ot, xall)
 
 
+def put_kernel(a, b, c, ao, bo, co, sems):
+    copies = [
+        pltpu.make_async_copy(src, dst, sems.at[t])
+        for t, (src, dst) in enumerate(((c, co), (a, ao), (b, bo)))
+    ]
+    for copy in copies:
+        copy.start()
+    for copy in copies:
+        copy.wait()
+
+
+def put(a, b, c):
+    vm = pl.BlockSpec(memory_space=pltpu.VMEM)
+    hbm = pl.BlockSpec(memory_space=pltpu.HBM)
+    return pl.pallas_call(
+        put_kernel,
+        out_shape=tuple(jax.ShapeDtypeStruct(t.shape, t.dtype) for t in (a, b, c)),
+        in_specs=[vm, vm, vm],
+        out_specs=(hbm, hbm, hbm),
+        scratch_shapes=[pltpu.SemaphoreType.DMA((3,))],
+        compiler_params=pltpu.CompilerParams(vmem_limit_bytes=4 * 1024 * 1024),
+        name="put",
+    )(a, b, c)
+
+
 def local(node_feats, qkv_weight, block_pairs, grad_out):
-    xall, b1, b2, kv, kvt = gather(node_feats, qkv_weight, grad_out)
-    ot, dproj = attention(block_pairs.reshape(-1), b1, b2, kv, kvt)
-    return scatter(dproj, qkv_weight, ot, xall.reshape(NB * BLOCK, D))
+    operands = (node_feats, qkv_weight, grad_out, jnp.transpose(block_pairs[0]))
+    held = [pltpu.with_memory_space_constraint(t, pltpu.HBM) for t in operands]
+    xall, b1, b2, kv, kvt, lst = gather(*held)
+    ot, dproj = attention(lst, b1, b2, kv, kvt)
+    return put(*scatter(dproj, qkv_weight, ot, xall.reshape(NB * BLOCK, D)))
 
 
 def solution(mesh):

time: 147 us -> 135 us (0.918)
  local copies, waits for them, and re-layouts: 12.8 us -> 0.01 us
  Pallas kernels: 133 us -> 135 us
    unnamed x16 -> x2, local copies, waits for them, and re-layouts: 12.7 us -> 0.01 us
    pallas_call x1, Pallas kernels: 50.8 us -> 55.3 us  [scatter(): pl.pallas_call(scatter_kernel, out_shape=(jax.ShapeDtypeStruct((1, BLOCK,...]
    pallas_call x1, Pallas kernels: 52.5 us -> 49.3 us  [gather(): pl.pallas_call(gather_kernel, out_shape=(jax.ShapeDtypeStruct((NB, BLOCK,...]
where the time goes in v2:
time: 135 us
  Pallas kernels  135 us (100%)
    pallas_call x1, Pallas kernels, scatter(): pl.pallas_call(scatter_kernel, out_shape=(jax.ShapeDtypeStruct((1, BLOCK,...  55.3 us
    pallas_call x1, Pallas kernels, gather(): pl.pallas_call(gather_kernel, out_shape=(jax.ShapeDtypeStruct((NB, BLOCK,...  49.3 us
    pallas_call x1, Pallas kernels, attention(): pl.pallas_call(attn_kernel, out_shape=(jax.ShapeDtypeStruct((NB, HD, BLOC...  28.9 us

profile of v2, /device:TPU:1, one launch (start us, length us, event | category | flops | bytes accessed | tf_op | source)
XLA Modules:
  0.0 135.3 jit_solution(830662555364609387)
XLA Ops:
  0.6 0.0 copy-start
  0.6 49.3 %gather_project.1 = (bf16[16,128,1024]{2,1,0:T(8,128)(2,1)S(1)}, bf16[16,128,256]{2,1,0:T(8,128)(2,1)S(1)}, bf16[16,256,128]{2,1,0:T(8,128)(2,1)S(1)}, bf16[2048...) custom-call(bf16[1,128,1024]{2,1,0:T(8,128)(2,1)} %x.1, bf16[192,1024]{1,0:T(8,128)(2,1)} %w_hbm.3, ...), custom_call_target="tpu_custom_call" | custom-call | tf_op jit(solution)/shard_map/gather_project/pallas_call | solution.py:366
  50.0 28.9 %attention.1 = (bf16[16,64,128]{2,1,0:T(8,128)(2,1)S(1)}, bf16[2048,192]{1,0:T(8,128)(2,1)S(1)}) custom-call(s32[16,128]{1,0:T(8,128)S(1)} %get-tuple-element.14.lst, bf16[16,128,256]{2,1,0:T(8,128)(2,1)S(1)} %get-tuple-element.15.b1, bf16[16,256,128]{2,1,0:T(8,128)(2,1)S(1)} %get-tuple-element.16.b2, bf16[2048,128]{1,0:T(8,128)(2,1)S(1)} %get-tuple-element.17.kv, ...), custom_call_target="tpu_custom_call" | custom-call | tf_op jit(solution)/shard_map/attention/pallas_call | solution.py:121
  78.9 0.0 copy-done
  78.9 55.3 %scatter_reduce.1 = (bf16[1,128,1024]{2,1,0:T(8,128)(2,1)S(1)}, bf16[1,128,1024]{2,1,0:T(8,128)(2,1)S(1)}, f32[192,1024]{1,0:T(8,128)S(1)}) custom-call(bf16[2048,192]{1,0:T(8,128)(2,1)S(1)} %get-tuple-element.19.dproj, bf16[192,1024]{1,0:T(8,128)(2,1)S(1)} %copy-done, bf16[16,64,128]{2,1,0:T(8,128)(2,1)S(1)} %get-tuple-element.20.ot, ...), custom_call_target="tpu_custom_call" | custom-call | tf_op jit(solution)/shard_map/scatter_reduce/pallas_call | solution.py:640
  134.2 1.1 put.1
Async XLA Ops:
  0.6 78.3 %copy-start = (bf16[192,1024]{1,0:T(8,128)(2,1)S(1)}, bf16[192,1024]{1,0:T(8,128)(2,1)}, u32[]{:S(2)}) copy-start(bf16[192,1024]{1,0:T(8,128)(2,1)} %w_hbm.3) | copy-start | bytes 1179652

commit v3 on v2

--- a/solution.py
+++ b/solution.py
@@ -12,8 +12,7 @@
 HD = 64
 BLOCK = 128
 NB = 16
-CH = 4
-ROWS = CH * BLOCK
+BIG = True
 PAD = -1e30
 COUNT = 16
 ROWID = 17
@@ -26,85 +25,100 @@
     def at_block(j):
         return pl.ds(pl.multiple_of(j * BLOCK, BLOCK), BLOCK)
 
-    def at_chunk(c):
-        return pl.ds(pl.multiple_of(c * ROWS, ROWS), ROWS)
-
-    def chunks(r):
-        return lax.div(lst[r, COUNT] + (CH - 1), CH)
-
-    def scores(r, c, buf, w1, m):
+    def at_rows(base, ch):
+        return pl.ds(pl.multiple_of(base * BLOCK, BLOCK), ch * BLOCK)
+
+    def fold(v):
+        return v.reshape(v.shape[0] // 8, 8, BLOCK)
+
+    def scores(r, base, ch, buf, w1, m):
         n = lst[r, COUNT]
-        lhs = jnp.concatenate([kv[at_block(lst[r, c * CH + t]), :] for t in range(CH)], axis=0)
+        lhs = jnp.concatenate([kv[at_block(lst[r, base + t]), :] for t in range(ch)], axis=0)
         sd = jnp.dot(lhs, w1, preferred_element_type=F32)
         s = jnp.concatenate(
             [
                 sd[t * BLOCK : (t + 1) * BLOCK, :BLOCK]
-                + jnp.where(c * CH + t < n, 0.0, PAD).astype(F32)
-                for t in range(CH)
+                + jnp.where(base + t < n, 0.0, PAD).astype(F32)
+                for t in range(ch)
             ],
             axis=0,
         )
-        s_scr[buf, at_chunk(c), :] = s
-        d_scr[buf, at_chunk(c), :] = sd[:, BLOCK:]
-        return jnp.maximum(m, jnp.max(s.reshape(ROWS // 8, 8, BLOCK), axis=0))
-
-    def weigh(r, buf, m):
-        m = jnp.max(m, axis=0, keepdims=True)
-
-        def step(c, carry):
-            l, d = carry
-            e = jnp.exp2((s_scr[buf, at_chunk(c), :] - m) * SCALE)
-            s_scr[buf, at_chunk(c), :] = e
-            l = l + jnp.sum(e.reshape(ROWS // 8, 8, BLOCK), axis=0)
-            ed = e * d_scr[buf, at_chunk(c), :]
-            d = d + jnp.sum(ed.reshape(ROWS // 8, 8, BLOCK), axis=0)
-            return l, d
-
-        zero = jnp.zeros((8, BLOCK), F32)
-        l, d = lax.fori_loop(0, chunks(r), step, (zero, zero))
-        linv = 1.0 / jnp.sum(l, axis=0, keepdims=True)
-        return linv, jnp.sum(d, axis=0, keepdims=True) * linv
-
-    def gradients(r, c, buf, w2, linv, delta, oq):
-        e = s_scr[buf, at_chunk(c), :]
-        p = e * linv
-        ds = p * ((d_scr[buf, at_chunk(c), :] - delta) * 0.125)
+        s_scr[buf, at_rows(base, ch), :] = s
+        d_scr[buf, at_rows(base, ch), :] = sd[:, BLOCK:]
+        return jnp.maximum(m, jnp.max(fold(s), axis=0))
+
+    def weigh(base, ch, buf, m, l, d):
+        e = jnp.exp2((s_scr[buf, at_rows(base, ch), :] - m) * SCALE)
+        s_scr[buf, at_rows(base, ch), :] = e
+        l = l + jnp.sum(fold(e), axis=0)
+        d = d + jnp.sum(fold(e * d_scr[buf, at_rows(base, ch), :]), axis=0)
+        return l, d
+
+    def gradients(r, base, ch, buf, w2, linv, delta, oq):
+        p = s_scr[buf, at_rows(base, ch), :] * linv
+        ds = p * ((d_scr[buf, at_rows(base, ch), :] - delta) * 0.125)
         cat = jnp.concatenate([ds.astype(BF), p.astype(BF)], axis=1)
-        cols = [lst[r, c * CH + t] for t in range(CH)]
+        cols = [lst[r, base + t] for t in range(ch)]
         lhs = jnp.concatenate([kvt[:, at_block(j)] for j in cols], axis=1)
         oq = oq + jnp.dot(lhs, cat, preferred_element_type=F32)
         g = jnp.dot(cat, w2, preferred_element_type=F32)
-        for t in range(CH):
+        for t in range(ch):
             acc[at_block(cols[t]), :] += g[t * BLOCK : (t + 1) * BLOCK]
         return oq
 
+    def sweep(r, body, state):
+        n = lst[r, COUNT]
+        n8 = lax.div(n + 3, 8)
+        n4 = lax.div(n + 3, 4) - 2 * n8
+        if BIG:
+            state = lax.fori_loop(0, n8, lambda c, st: body(c * 8, 8, st), state)
+            return lax.fori_loop(0, n4, lambda c, st: body(n8 * 8, 4, st), state)
+        return lax.fori_loop(0, lax.div(n + 3, 4), lambda c, st: body(c * 4, 4, st), state)
+
+    def rows_max(m):
+        return jnp.max(m, axis=0, keepdims=True)
+
+    def close(l, d):
+        linv = 1.0 / jnp.sum(l, axis=0, keepdims=True)
+        return linv, jnp.sum(d, axis=0, keepdims=True) * linv
+
     low = jnp.full((8, BLOCK), PAD, F32)
-    first = b1[lst[0, ROWID]]
-    m0 = lax.fori_loop(0, chunks(0), lambda c, m: scores(0, c, 0, first, m), low)
-    linv0, delta0 = weigh(0, 0, m0)
+    zero = jnp.zeros((8, BLOCK), F32)
+    w1_0 = b1[lst[0, ROWID]]
+    w1_1 = b1[lst[1, ROWID]]
+    m0 = rows_max(sweep(0, lambda b, ch, m: scores(0, b, ch, 0, w1_0, m), low))
+
+    def second(b, ch, st):
+        m, l, d = st
+        m = scores(1, b, ch, 1, w1_1, m)
+        l, d = weigh(b, ch, 0, m0, l, d)
+        return m, l, d
+
+    m1, l0, d0 = sweep(0, second, (low, zero, zero))
 
     def row(r, carry):
-        linv, delta = carry
+        linv, delta, m = carry
+        m = rows_max(m)
         i = lst[r, ROWID]
-        buf = lax.rem(r, 2)
-        nxt = jnp.minimum(r + 1, NB - 1)
-        w1 = b1[lst[nxt, ROWID]]
+        far = jnp.minimum(r + 2, NB - 1)
+        w1 = b1[lst[far, ROWID]]
         w2 = b2[i]
-
-        def both(c, state):
-            oq, m = state
-            m = scores(nxt, c, 1 - buf, w1, m)
-            oq = gradients(r, c, buf, w2, linv, delta, oq)
-            return oq, m
-
-        oq, m = lax.fori_loop(
-            0, chunks(r), both, (jnp.zeros((BLOCK, 2 * BLOCK), F32), low)
-        )
+        buf, buf1, buf2 = lax.rem(r, 3), lax.rem(r + 1, 3), lax.rem(r + 2, 3)
+
+        def body(b, ch, st):
+            oq, l, d, mf = st
+            mf = scores(far, b, ch, buf2, w1, mf)
+            l, d = weigh(b, ch, buf1, m, l, d)
+            oq = gradients(r, b, ch, buf, w2, linv, delta, oq)
+            return oq, l, d, mf
+
+        oq, l, d, mf = sweep(r, body, (jnp.zeros((BLOCK, 2 * BLOCK), F32), zero, zero, low))
         ot[i] = oq[HD:, BLOCK:].astype(BF)
         dproj[at_block(i), 0:BLOCK] = oq[:, :BLOCK].T.astype(BF)
-        return weigh(nxt, 1 - buf, m)
-
-    lax.fori_loop(0, NB, row, (linv0, delta0))
+        linv, delta = close(l, d)
+        return linv, delta, mf
+
+    lax.fori_loop(0, NB, row, (*close(l0, d0), m1))
 
     def fin(i, _):
         a = acc[at_block(i), :].astype(BF)
@@ -127,11 +141,11 @@
         in_specs=[pl.BlockSpec(memory_space=pltpu.SMEM), vm, vm, vm, vm],
         out_specs=(vm, vm),
         scratch_shapes=[
-            pltpu.VMEM((2, n, BLOCK), F32),
-            pltpu.VMEM((2, n, BLOCK), F32),
+            pltpu.VMEM((3, n, BLOCK), F32),
+            pltpu.VMEM((3, n, BLOCK), F32),
             pltpu.VMEM((n, BLOCK), F32),
         ],
-        compiler_params=pltpu.CompilerParams(vmem_limit_bytes=12 * 1024 * 1024),
+        compiler_params=pltpu.CompilerParams(vmem_limit_bytes=14 * 1024 * 1024),
         name="attention",
     )(lst, b1, b2, kv, kvt)
 
@@ -523,12 +537,9 @@
     other = pl.ds(pl.multiple_of((1 - cc) * hrow, QUART), hrow)
     wide = D // NX
 
-    def stage0a():
+    def stage0():
         lax.fori_loop(0, NB, turn, 0)
-        lax.fori_loop(0, 2, wstep, 0)
-
-    def stage0b():
-        lax.fori_loop(2, D // 256, wstep, 0)
+        lax.fori_loop(0, D // 256, wstep, 0)
         cs[...] = dwf[other, :].astype(BF)
         go(rcopy(cs, cr, sc.at[0], rc.at[0], sib))
 
@@ -593,35 +604,34 @@
     asteps(0)
     for flow in (4, 5, 2, 3):
         zstep(flow, 1)
+    stage0()
     ysend(2)
     ysend(-2)
-    stage0a()
     asteps(1)
+    stage1()
     for flow in (4, 5, 2, 3):
         zstep(flow, 2)
     ysend(1)
     ysend(-1)
-    stage0b()
+    stage2()
     asteps(2)
-    stage1()
     for flow in (4, 5, 2, 3):
         zstep(flow, 3)
     ysend(0)
-    stage2()
-    asteps(3)
-    ysb[8] = total(4, p, HALF).astype(BF)
-    go(ymsg(8))
-    stage3()
-    own_b = total(2, y, HALF)
-    stage4()
-    ymsg(0).wait_recv()
-    ng[0, :HALF, :] = (total(0, y, 0) + yrb[0].astype(F32)).astype(BF)
     for d in range(1, NB):
         frm = lax.rem(s + NB - d, NB)
         rcopy(ot.at[s], arecv.at[frm], sa.at[d - 1], ra.at[d - 1], {"seq": frm}).wait_recv()
     for c in range(NB // 2):
         t = jnp.concatenate([arecv[2 * c], arecv[2 * c + 1]], axis=0).astype(F32)
         att[0, :, c * BLOCK : (c + 1) * BLOCK] = t.T.astype(BF)
+    stage3()
+    asteps(3)
+    stage4()
+    ysb[8] = total(4, p, HALF).astype(BF)
+    go(ymsg(8))
+    own_b = total(2, y, HALF)
+    ymsg(0).wait_recv()
+    ng[0, :HALF, :] = (total(0, y, 0) + yrb[0].astype(F32)).astype(BF)
     stage5()
     ymsg(8).wait_recv()
     ng[0, HALF:, :] = (own_b + yrb[8].astype(F32)).astype(BF)

time: 135 us -> 126 us (0.933); the launches traced: 135 us -> 124 us
  Pallas kernels: 135 us -> 124 us
    pallas_call x1, Pallas kernels: 55.3 us -> 48.3 us  [scatter(): pl.pallas_call(scatter_kernel, out_shape=(jax.ShapeDtypeStruct((1, BLOCK,...]
    pallas_call x1, Pallas kernels: 28.9 us -> 25 us  [attention(): pl.pallas_call(attn_kernel, out_shape=(jax.ShapeDtypeStruct((NB, HD, BLOC...]
where the time goes in v3:
time: 126 us; the launch traced here: 124 us
  Pallas kernels  124 us (98%)
    pallas_call x1, Pallas kernels, gather(): pl.pallas_call(gather_kernel, out_shape=(jax.ShapeDtypeStruct((NB, BLOCK,...  49.3 us
    pallas_call x1, Pallas kernels, scatter(): pl.pallas_call(scatter_kernel, out_shape=(jax.ShapeDtypeStruct((1, BLOCK,...  48.3 us
    pallas_call x1, Pallas kernels, attention(): pl.pallas_call(attn_kernel, out_shape=(jax.ShapeDtypeStruct((NB, HD, BLOC...  25 us

profile of v3, /device:TPU:1, one launch (start us, length us, event | category | flops | bytes accessed | tf_op | source)
XLA Modules:
  0.0 124.3 jit_solution(13701981930234217373)
XLA Ops:
  0.6 0.0 copy-start
  0.6 49.3 %gather_project.1 = (bf16[16,128,1024]{2,1,0:T(8,128)(2,1)S(1)}, bf16[16,128,256]{2,1,0:T(8,128)(2,1)S(1)}, bf16[16,256,128]{2,1,0:T(8,128)(2,1)S(1)}, bf16[2048...) custom-call(bf16[1,128,1024]{2,1,0:T(8,128)(2,1)} %x.1, bf16[192,1024]{1,0:T(8,128)(2,1)} %w_hbm.3, ...), custom_call_target="tpu_custom_call" | custom-call | tf_op jit(solution)/shard_map/gather_project/pallas_call | solution.py:380
  50.0 25.0 %attention.1 = (bf16[16,64,128]{2,1,0:T(8,128)(2,1)S(1)}, bf16[2048,192]{1,0:T(8,128)(2,1)S(1)}) custom-call(s32[16,128]{1,0:T(8,128)S(1)} %get-tuple-element.14.lst, bf16[16,128,256]{2,1,0:T(8,128)(2,1)S(1)} %get-tuple-element.15.b1, bf16[16,256,128]{2,1,0:T(8,128)(2,1)S(1)} %get-tuple-element.16.b2, bf16[2048,128]{1,0:T(8,128)(2,1)S(1)} %get-tuple-element.17.kv, ...), custom_call_target="tpu_custom_call" | custom-call | tf_op jit(solution)/shard_map/attention/pallas_call | solution.py:135
  75.0 0.0 copy-done
  75.0 48.3 %scatter_reduce.1 = (bf16[1,128,1024]{2,1,0:T(8,128)(2,1)S(1)}, bf16[1,128,1024]{2,1,0:T(8,128)(2,1)S(1)}, f32[192,1024]{1,0:T(8,128)S(1)}) custom-call(bf16[2048,192]{1,0:T(8,128)(2,1)S(1)} %get-tuple-element.19.dproj, bf16[192,1024]{1,0:T(8,128)(2,1)S(1)} %copy-done, bf16[16,64,128]{2,1,0:T(8,128)(2,1)S(1)} %get-tuple-element.20.ot, ...), custom_call_target="tpu_custom_call" | custom-call | tf_op jit(solution)/shard_map/scatter_reduce/pallas_call | solution.py:650
  123.3 1.1 put.1
Async XLA Ops:
  0.6 74.4 %copy-start = (bf16[192,1024]{1,0:T(8,128)(2,1)S(1)}, bf16[192,1024]{1,0:T(8,128)(2,1)}, u32[]{:S(2)}) copy-start(bf16[192,1024]{1,0:T(8,128)(2,1)} %w_hbm.3) | copy-start | bytes 1179652

commit v4 on v3

--- a/solution.py
+++ b/solution.py
@@ -173,10 +173,12 @@
     return s, y, z
 
 
-def greet(peers):
+def greet(peers, meanwhile=None):
     barrier = pltpu.get_barrier_semaphore()
     for peer in peers:
         pl.semaphore_signal(barrier, inc=1, device_id=peer, device_id_type=MESH)
+    if meanwhile is not None:
+        meanwhile()
     pl.semaphore_wait(barrier, len(peers))
 
 
@@ -215,7 +217,7 @@
 def gather_kernel(
     x, w_hbm, g_hbm, pairs_hbm,
     xall, b1, b2, kv, kvt, lst,
-    w, g, pairs, xg, gsend, grecv, sz, rz, sy, ry, sg, rg, lx, ll,
+    w, g, pairs, xg, gsend, grecv, sz, rz, sy, ry, sg, rg, lx, ll, hop,
 ):
     s, y, z = ring_place()
     p = 1 - y
@@ -230,7 +232,14 @@
     load_g.start()
     load_w.start()
     load_p.start()
-    greet([{"seq": lax.rem(s + d, NB)} for d in range(1, NB)])
+    near = [up, down, across]
+    greet(near)
+
+    def relay(r):
+        for peer in near:
+            pl.semaphore_signal(hop.at[r], inc=1, device_id=peer, device_id_type=MESH)
+        pl.semaphore_wait(hop.at[r], len(near))
+
     load.wait()
 
     def block(col, off):
@@ -290,6 +299,7 @@
         c.start()
         outs.append(c)
 
+    relay(0)
     load_g.wait()
     for c in range(NB // 2):
         t = g[:, c * BLOCK : (c + 1) * BLOCK].astype(F32).T.astype(BF)
@@ -307,11 +317,14 @@
             device_id_type=MESH,
         )
 
+    relay(1)
     load_w.wait()
     compute(s, 0)
+    relay(2)
     ymsg(8, p, False).wait_recv()
     for flow in (4, 5):
         sent.append(zmsg(flow, 0, 0, True))
+    relay(3)
     for d in range(1, NB):
         c = gmsg(d)
         c.start()
@@ -404,6 +417,7 @@
             sem((NB - 1,)),
             sem((NB,)),
             sem((4,)),
+            pltpu.SemaphoreType.REGULAR((4,)),
         ],
         compiler_params=pltpu.CompilerParams(
             collective_id=0, has_side_effects=True, vmem_limit_bytes=20 * 1024 * 1024
@@ -413,10 +427,10 @@
 
 
 def scatter_kernel(
-    dproj, w_hbm, ot, xv,
+    dproj, w, ot, xv,
     att, ng, wg,
-    w, zs, zr, ysb, yrb, arecv, dt, dwf, cs, cr, xs, xr, hs, hr, fs, fo, fsib,
-    sz, rz, sy, ry, sa, ra, sc, rc, sx, rx, sh, rh, sf, rf, lx,
+    px, zs, zr, ysb, yrb, arecv, dt, dwf, cs, cr, xs, xr, hs, hr, fs, fo, fsib,
+    sz, rz, sy, ry, sa, ra, sc, rc, sx, rx, sh, rh, sf, rf,
 ):
     s, y, z = ring_place()
     p = 1 - y
@@ -435,13 +449,21 @@
     def hpeer(d):
         return {"clus": cx * (NY * CORES) + lax.rem(ch + d, NY) * CORES + cc}
 
-    load = pltpu.make_async_copy(w_hbm, w, lx)
-    load.start()
+    def terms():
+        def step(t, _):
+            at = pl.ds(pl.multiple_of(t * 256, 256), 256)
+            px[:, at] = jnp.dot(dproj[...], w[:, at], preferred_element_type=F32).astype(BF)
+            return 0
+
+        lax.fori_loop(0, D // 256, step, 0)
+        arecv[s] = ot[s]
+
     greet(
         [{"seq": lax.rem(s + d, NB)} for d in range(1, NB)]
         + [sib]
         + [xpeer(d) for d in range(1, NX)]
-        + [hpeer(d) for d in range(1, NY)]
+        + [hpeer(d) for d in range(1, NY)],
+        terms,
     )
 
     def block(col, off):
@@ -449,8 +471,7 @@
 
     def part(col, off, first, rows):
         b = block(col, off)
-        at = pl.ds(pl.multiple_of(b * BLOCK + first, QUART), rows)
-        return jnp.dot(dproj[at, :], w[...], preferred_element_type=F32)
+        return px.at[pl.ds(pl.multiple_of(b * BLOCK + first, QUART), rows), :]
 
     sent = []
 
@@ -467,13 +488,18 @@
 
     def zmsg(flow, k):
         at = span(flow, k)
+        src = zs.at[flow, k, at]
+        if k == 0 and flow >= 2:
+            lo = QUART if flow % 2 else 0
+            src = part(p if flow >= 4 else y, 4, HALF + lo, QUART)
         return rcopy(
-            zs.at[flow, k, at], zr.at[flow, k, at], sz.at[flow, k], rz.at[flow, k],
+            src, zr.at[flow, k, at], sz.at[flow, k], rz.at[flow, k],
             down if flow % 2 else up,
         )
 
     def ymsg(idx):
-        return rcopy(ysb.at[idx], yrb.at[idx], sy.at[idx], ry.at[idx], across)
+        src = ysb if idx == 8 else part(p, idx, 0, HALF)
+        return rcopy(src, yrb.at[idx], sy.at[idx], ry.at[idx], across)
 
     def go(c):
         c.start()
@@ -483,19 +509,18 @@
         col = p if flow >= 4 else y
         base = 0 if flow < 2 else HALF
         off = (4 - k) * (-1 if flow % 2 else 1)
+        lo = QUART if flow % 2 else 0
         if k == 0:
-            lo = QUART if flow % 2 else 0
-            val = part(col, off, base + lo, QUART)
             if flow < 2:
+                val = part(col, off, lo, QUART)[...].astype(F32)
                 val = val + yrb[off % NZ, lo : lo + QUART, :].astype(F32)
-            zs[flow, 0, lo : lo + QUART, :] = val.astype(BF)
+                zs[flow, 0, lo : lo + QUART, :] = val.astype(BF)
         else:
-            val = part(col, off, base, HALF)
+            val = part(col, off, base, HALF)[...].astype(F32)
             if flow < 2:
                 val = val + yrb[off % NZ].astype(F32)
             zmsg(flow, k - 1).wait_recv()
             if k == 1:
-                lo = QUART if flow % 2 else 0
                 zs[flow, 1, QUART - lo : HALF - lo, :] = val[QUART - lo : HALF - lo].astype(BF)
                 zs[flow, 1, lo : lo + QUART, :] = (
                     val[lo : lo + QUART] + zr[flow, 0, lo : lo + QUART, :].astype(F32)
@@ -505,10 +530,8 @@
         go(zmsg(flow, k))
 
     def ysend(off):
-        ysb[off % NZ] = part(p, off, 0, HALF).astype(BF)
         go(ymsg(off % NZ))
 
-    load.wait()
     for flow in (4, 5):
         zstep(flow, 0)
     ysend(4)
@@ -519,7 +542,6 @@
     for d in range(1, NB):
         to = lax.rem(s + d, NB)
         go(rcopy(ot.at[to], arecv.at[s], sa.at[d - 1], ra.at[d - 1], {"seq": to}))
-    arecv[s] = ot[s]
 
     def turn(t, _):
         at = pl.ds(pl.multiple_of(t * BLOCK, BLOCK), BLOCK)
@@ -595,7 +617,7 @@
         zstep(1, k)
 
     def total(flow, col, base):
-        val = part(col, 0, base, HALF)
+        val = part(col, 0, base, HALF)[...].astype(F32)
         for f in (flow, flow + 1):
             zmsg(f, 3).wait_recv()
             val = val + zr[f, 3].astype(F32)
@@ -627,7 +649,7 @@
     stage3()
     asteps(3)
     stage4()
-    ysb[8] = total(4, p, HALF).astype(BF)
+    ysb[...] = total(4, p, HALF).astype(BF)
     go(ymsg(8))
     own_b = total(2, y, HALF)
     ymsg(0).wait_recv()
@@ -641,7 +663,6 @@
 
 def scatter(dproj, w, ot, xall):
     vm = pl.BlockSpec(memory_space=pltpu.VMEM)
-    hbm = pl.BlockSpec(memory_space=pltpu.HBM)
     n = NB * BLOCK
     sem = pltpu.SemaphoreType.DMA
     vmem = pltpu.VMEM
@@ -654,13 +675,13 @@
             jax.ShapeDtypeStruct((1, BLOCK, D), BF),
             jax.ShapeDtypeStruct((3 * HD, D), F32),
         ),
-        in_specs=[vm, hbm, vm, vm],
+        in_specs=[vm, vm, vm, vm],
         out_specs=(vm, vm, vm),
         scratch_shapes=[
-            vmem((3 * HD, D), BF),
+            vmem((n, D), BF),
             vmem((6, 4, HALF, D), BF),
             vmem((6, 4, HALF, D), BF),
-            vmem((9, HALF, D), BF),
+            vmem((HALF, D), BF),
             vmem((9, HALF, D), BF),
             vmem((NB, HD, BLOCK), BF),
             vmem((3 * HD, n), BF),
@@ -688,10 +709,9 @@
             sem((NY - 1,)),
             sem((NX - 1,)),
             sem((NX - 1,)),
-            sem,
         ],
         compiler_params=pltpu.CompilerParams(
-            collective_id=1, has_side_effects=True, vmem_limit_bytes=22 * 1024 * 1024
+            collective_id=1, has_side_effects=True, vmem_limit_bytes=24 * 1024 * 1024
         ),
         name="scatter_reduce",
     )(dproj, w, ot, xall)

time: 126 us -> 123 us (0.976)
  Pallas kernels: 124 us -> 121 us
    pallas_call x1, Pallas kernels: 48.3 us -> 45.1 us  [scatter(): pl.pallas_call(scatter_kernel, out_shape=(jax.ShapeDtypeStruct((1, BLOCK,...]
where the time goes in v4:
time: 123 us; the launch traced here: 122 us
  Pallas kernels  121 us (98%)
    pallas_call x1, Pallas kernels, gather(): pl.pallas_call(gather_kernel, out_shape=(jax.ShapeDtypeStruct((NB, BLOCK,...  49.5 us
    pallas_call x1, Pallas kernels, scatter(): pl.pallas_call(scatter_kernel, out_shape=(jax.ShapeDtypeStruct((1, BLOCK,...  45.1 us
    pallas_call x1, Pallas kernels, attention(): pl.pallas_call(attn_kernel, out_shape=(jax.ShapeDtypeStruct((NB, HD, BLOC...  25.3 us

profile of v4, /device:TPU:1, one launch (start us, length us, event | category | flops | bytes accessed | tf_op | source)
XLA Modules:
  0.0 121.6 jit_solution(6054021430702113915)
XLA Ops:
  0.6 0.0 copy-start
  0.6 49.5 %gather_project.1 = (bf16[16,128,1024]{2,1,0:T(8,128)(2,1)S(1)}, bf16[16,128,256]{2,1,0:T(8,128)(2,1)S(1)}, bf16[16,256,128]{2,1,0:T(8,128)(2,1)S(1)}, bf16[2048...) custom-call(bf16[1,128,1024]{2,1,0:T(8,128)(2,1)} %x.1, bf16[192,1024]{1,0:T(8,128)(2,1)} %w.1, ...), custom_call_target="tpu_custom_call" | custom-call | tf_op jit(solution)/shard_map/gather_project/pallas_call | solution.py:393
  50.1 25.3 %attention.1 = (bf16[16,64,128]{2,1,0:T(8,128)(2,1)S(1)}, bf16[2048,192]{1,0:T(8,128)(2,1)S(1)}) custom-call(s32[16,128]{1,0:T(8,128)S(1)} %get-tuple-element.14.lst, bf16[16,128,256]{2,1,0:T(8,128)(2,1)S(1)} %get-tuple-element.15.b1, bf16[16,256,128]{2,1,0:T(8,128)(2,1)S(1)} %get-tuple-element.16.b2, bf16[2048,128]{1,0:T(8,128)(2,1)S(1)} %get-tuple-element.17.kv, ...), custom_call_target="tpu_custom_call" | custom-call | tf_op jit(solution)/shard_map/attention/pallas_call | solution.py:135
  75.4 0.0 copy-done
  75.4 45.1 %scatter_reduce.1 = (bf16[1,128,1024]{2,1,0:T(8,128)(2,1)S(1)}, bf16[1,128,1024]{2,1,0:T(8,128)(2,1)S(1)}, f32[192,1024]{1,0:T(8,128)S(1)}) custom-call(bf16[2048,192]{1,0:T(8,128)(2,1)S(1)} %get-tuple-element.19.dproj, bf16[192,1024]{1,0:T(8,128)(2,1)S(1)} %copy-done, bf16[16,64,128]{2,1,0:T(8,128)(2,1)S(1)} %get-tuple-element.20.ot, ...), custom_call_target="tpu_custom_call" | custom-call | tf_op jit(solution)/shard_map/scatter_reduce/pallas_call | solution.py:671
  120.5 1.1 put.1
Async XLA Ops:
  0.6 74.8 %copy-start = (bf16[192,1024]{1,0:T(8,128)(2,1)S(1)}, bf16[192,1024]{1,0:T(8,128)(2,1)}, u32[]{:S(2)}) copy-start(bf16[192,1024]{1,0:T(8,128)(2,1)} %w.1) | copy-start | bytes 1179652

commit v5 on v4

--- a/solution.py
+++ b/solution.py
@@ -12,14 +12,14 @@
 HD = 64
 BLOCK = 128
 NB = 16
-BIG = True
+SIZES = (1, 2, 4, 6, 8, 10, 12, 14, 16)
 PAD = -1e30
 COUNT = 16
 ROWID = 17
 SCALE = 0.125 * math.log2(math.e)
 
 
-def attn_kernel(lst, b1, b2, kv, kvt, ot, dproj, s_scr, d_scr, acc):
+def attn_kernel(lst, b1, b2, kv, ot, dproj, s_scr, d_scr, acc):
     acc[...] = jnp.zeros_like(acc)
 
     def at_block(j):
@@ -59,8 +59,8 @@
         ds = p * ((d_scr[buf, at_rows(base, ch), :] - delta) * 0.125)
         cat = jnp.concatenate([ds.astype(BF), p.astype(BF)], axis=1)
         cols = [lst[r, base + t] for t in range(ch)]
-        lhs = jnp.concatenate([kvt[:, at_block(j)] for j in cols], axis=1)
-        oq = oq + jnp.dot(lhs, cat, preferred_element_type=F32)
+        rhs = jnp.concatenate([kv[at_block(j), :] for j in cols], axis=0)
+        oq = oq + lax.dot_general(cat, rhs, (((0,), (0,)), ((), ())), preferred_element_type=F32)
         g = jnp.dot(cat, w2, preferred_element_type=F32)
         for t in range(ch):
             acc[at_block(cols[t]), :] += g[t * BLOCK : (t + 1) * BLOCK]
@@ -68,12 +68,11 @@
 
     def sweep(r, body, state):
         n = lst[r, COUNT]
-        n8 = lax.div(n + 3, 8)
-        n4 = lax.div(n + 3, 4) - 2 * n8
-        if BIG:
-            state = lax.fori_loop(0, n8, lambda c, st: body(c * 8, 8, st), state)
-            return lax.fori_loop(0, n4, lambda c, st: body(n8 * 8, 4, st), state)
-        return lax.fori_loop(0, lax.div(n + 3, 4), lambda c, st: body(c * 4, 4, st), state)
+        which = 0
+        for size in SIZES[:-1]:
+            which = which + (n > size).astype(jnp.int32)
+        arms = [lambda st, ch=ch: body(0, ch, st) for ch in SIZES]
+        return lax.switch(which, arms, state)
 
     def rows_max(m):
         return jnp.max(m, axis=0, keepdims=True)
@@ -112,9 +111,9 @@
             oq = gradients(r, b, ch, buf, w2, linv, delta, oq)
             return oq, l, d, mf
 
-        oq, l, d, mf = sweep(r, body, (jnp.zeros((BLOCK, 2 * BLOCK), F32), zero, zero, low))
-        ot[i] = oq[HD:, BLOCK:].astype(BF)
-        dproj[at_block(i), 0:BLOCK] = oq[:, :BLOCK].T.astype(BF)
+        oq, l, d, mf = sweep(r, body, (jnp.zeros((2 * BLOCK, BLOCK), F32), zero, zero, low))
+        ot[i] = oq[BLOCK:, :].T[HD:].astype(BF)
+        dproj[at_block(i), 0:BLOCK] = oq[:BLOCK, :].astype(BF)
         linv, delta = close(l, d)
         return linv, delta, mf
 
@@ -129,7 +128,7 @@
     lax.fori_loop(0, NB, fin, 0, unroll=4)
 
 
-def attention(lst, b1, b2, kv, kvt):
+def attention(lst, b1, b2, kv):
     vm = pl.BlockSpec(memory_space=pltpu.VMEM)
     n = NB * BLOCK
     return pl.pallas_call(
@@ -138,7 +137,7 @@
             jax.ShapeDtypeStruct((NB, HD, BLOCK), BF),
             jax.ShapeDtypeStruct((n, 3 * HD), BF),
         ),
-        in_specs=[pl.BlockSpec(memory_space=pltpu.SMEM), vm, vm, vm, vm],
+        in_specs=[pl.BlockSpec(memory_space=pltpu.SMEM), vm, vm, vm],
         out_specs=(vm, vm),
         scratch_shapes=[
             pltpu.VMEM((3, n, BLOCK), F32),
@@ -147,7 +146,7 @@
         ],
         compiler_params=pltpu.CompilerParams(vmem_limit_bytes=14 * 1024 * 1024),
         name="attention",
-    )(lst, b1, b2, kv, kvt)
+    )(lst, b1, b2, kv)
 
 MESH = pl.DeviceIdType.MESH
 HD = 64
@@ -216,7 +215,7 @@
 
 def gather_kernel(
     x, w_hbm, g_hbm, pairs_hbm,
-    xall, b1, b2, kv, kvt, lst,
+    xall, b1, b2, kv, lst,
     w, g, pairs, xg, gsend, grecv, sz, rz, sy, ry, sg, rg, lx, ll, hop,
 ):
     s, y, z = ring_place()
@@ -226,11 +225,13 @@
     across = {"seq": p * NZ + z}
     load = pltpu.make_async_copy(x.at[0], xg.at[s], ll.at[0])
     load_g = pltpu.make_async_copy(g_hbm.at[0], g, ll.at[1])
-    load_w = pltpu.make_async_copy(w_hbm, w, ll.at[2])
+    load_w = pltpu.make_async_copy(w_hbm.at[pl.ds(HD, BLOCK)], w.at[pl.ds(0, BLOCK)], ll.at[2])
+    load_q = pltpu.make_async_copy(w_hbm.at[pl.ds(0, HD)], w.at[pl.ds(BLOCK, HD)], ll.at[4])
     load_p = pltpu.make_async_copy(pairs_hbm, pairs, ll.at[3])
     load.start()
     load_g.start()
     load_w.start()
+    load_q.start()
     load_p.start()
     near = [up, down, across]
     greet(near)
@@ -288,13 +289,11 @@
     def compute(b, n):
         xb = xg[b]
         at = pl.ds(pl.multiple_of(b * BLOCK, BLOCK), BLOCK)
-        kvf = dot_t(xb, w[HD:, :])
-        qt = dot_t(w[:HD, :], xb)
-        zero = jnp.zeros((HD, BLOCK), F32)
-        kv[at, :] = kvf.astype(BF)
-        kvt[:, at] = kvf.T.astype(BF)
-        b1[b, :HD, :] = jnp.concatenate([qt, zero], axis=1).astype(BF)
-        b2[b, :BLOCK, :] = jnp.concatenate([qt, zero], axis=0).T.astype(BF)
+        proj = dot_t(xb, w[...])
+        q = jnp.concatenate([proj[:, BLOCK:], jnp.zeros((BLOCK, HD), F32)], axis=1)
+        kv[at, :] = proj[:, :BLOCK].astype(BF)
+        b1[b, :HD, :] = jnp.concatenate([q.T[:HD], jnp.zeros((HD, BLOCK), F32)], axis=1).astype(BF)
+        b2[b, :BLOCK, :] = q.astype(BF)
         c = pltpu.make_async_copy(xg.at[b], xall.at[b], lx.at[n])
         c.start()
         outs.append(c)
@@ -319,6 +318,7 @@
 
     relay(1)
     load_w.wait()
+    load_q.wait()
     compute(s, 0)
     relay(2)
     ymsg(8, p, False).wait_recv()
@@ -397,11 +397,10 @@
             jax.ShapeDtypeStruct((NB, BLOCK, 2 * BLOCK), BF),
             jax.ShapeDtypeStruct((NB, 2 * BLOCK, BLOCK), BF),
             jax.ShapeDtypeStruct((n, BLOCK), BF),
-            jax.ShapeDtypeStruct((BLOCK, n), BF),
             jax.ShapeDtypeStruct((NB, BLOCK), jnp.int32),
         ),
         in_specs=[hbm, hbm, hbm, hbm],
-        out_specs=(anyw, vm, vm, vm, vm, vm),
+        out_specs=(anyw, vm, vm, vm, vm),
         scratch_shapes=[
             pltpu.VMEM((3 * HD, D), BF),
             pltpu.VMEM((BLOCK, D), BF),
@@ -416,7 +415,7 @@
             sem((NB - 1,)),
             sem((NB - 1,)),
             sem((NB,)),
-            sem((4,)),
+            sem((5,)),
             pltpu.SemaphoreType.REGULAR((4,)),
         ],
         compiler_params=pltpu.CompilerParams(
@@ -745,8 +744,8 @@
 def local(node_feats, qkv_weight, block_pairs, grad_out):
     operands = (node_feats, qkv_weight, grad_out, jnp.transpose(block_pairs[0]))
     held = [pltpu.with_memory_space_constraint(t, pltpu.HBM) for t in operands]
-    xall, b1, b2, kv, kvt, lst = gather(*held)
-    ot, dproj = attention(lst, b1, b2, kv, kvt)
+    xall, b1, b2, kv, lst = gather(*held)
+    ot, dproj = attention(lst, b1, b2, kv)
     return put(*scatter(dproj, qkv_weight, ot, xall.reshape(NB * BLOCK, D)))
 
 

time: 123 us -> 118 us (0.959)
  Pallas kernels: 121 us -> 115 us
    pallas_call x1, Pallas kernels: 25.3 us -> 19.4 us  [attention(): pl.pallas_call(attn_kernel, out_shape=(jax.ShapeDtypeStruct((NB, HD, BLOC...]
where the time goes in v5:
time: 118 us; the launch traced here: 117 us
  Pallas kernels  115 us (97%)
    pallas_call x1, Pallas kernels, gather(): pl.pallas_call(gather_kernel, out_shape=(jax.ShapeDtypeStruct((NB, BLOCK,...  49.6 us
    pallas_call x1, Pallas kernels, scatter(): pl.pallas_call(scatter_kernel, out_shape=(jax.ShapeDtypeStruct((1, BLOCK,...  44.9 us
    pallas_call x1, Pallas kernels, attention(): pl.pallas_call(attn_kernel, out_shape=(jax.ShapeDtypeStruct((NB, HD, BLOC...  19.4 us

profile of v5, /device:TPU:1, one launch (start us, length us, event | category | flops | bytes accessed | tf_op | source)
XLA Modules:
  0.0 116.8 jit_solution(1734479291038405867)
XLA Ops:
  0.6 49.6 %gather_project.1 = (bf16[16,128,1024]{2,1,0:T(8,128)(2,1)S(1)}, bf16[16,128,256]{2,1,0:T(8,128)(2,1)S(1)}, bf16[16,256,128]{2,1,0:T(8,128)(2,1)S(1)}, bf16[2048,128]{1,0:T(8,128)(2,1)S(1)}, s32[16,128]{1,0:T(8,128)S(1)}) custom-call(bf16[1,128,1024]{2,1,0:T(8,128)(2,1)} %x.1, bf16[192,1024]{1,0:T(8,128)(2,1)} %w.1, bf16[1,128,1024]{2,1,0:T(8,128)(2,1)} %g_hbm.1, ...), custom_call_target="tpu_custom_call" | custom-call | tf_op jit(solution)/shard_map/gather_project/pallas_call | solution.py:393
  50.3 19.4 %attention.1 = (bf16[16,64,128]{2,1,0:T(8,128)(2,1)S(1)}, bf16[2048,192]{1,0:T(8,128)(2,1)S(1)}) custom-call(s32[16,128]{1,0:T(8,128)S(1)} %get-tuple-element.13.lst, bf16[16,128,256]{2,1,0:T(8,128)(2,1)S(1)} %get-tuple-element.14.b1, bf16[16,256,128]{2,1,0:T(8,128)(2,1)S(1)} %get-tuple-element.15.b2, bf16[2048,128]{1,0:T(8,128)(2,1)S(1)} %get-tuple-element.16.kv), custom_call_target="tpu_custom_call" | custom-call | tf_op jit(solution)/shard_map/attention/pallas_call | solution.py:134
  69.6 0.0 copy-start
  69.7 1.0 copy-done
  70.6 44.9 %scatter_reduce.1 = (bf16[1,128,1024]{2,1,0:T(8,128)(2,1)S(1)}, bf16[1,128,1024]{2,1,0:T(8,128)(2,1)S(1)}, f32[192,1024]{1,0:T(8,128)S(1)}) custom-call(bf16[2048,192]{1,0:T(8,128)(2,1)S(1)} %get-tuple-element.17.dproj, bf16[192,1024]{1,0:T(8,128)(2,1)S(1)} %copy-done, bf16[16,64,128]{2,1,0:T(8,128)(2,1)S(1)} %get-tuple-element.18.ot, ...), custom_call_target="tpu_custom_call" | custom-call | tf_op jit(solution)/shard_map/scatter_reduce/pallas_call | solution.py:670
  115.6 1.1 put.1
Async XLA Ops:
  69.6 1.0 copy-start

commit v6 on v5

--- a/solution.py
+++ b/solution.py
@@ -56,7 +56,7 @@
 
     def gradients(r, base, ch, buf, w2, linv, delta, oq):
         p = s_scr[buf, at_rows(base, ch), :] * linv
-        ds = p * ((d_scr[buf, at_rows(base, ch), :] - delta) * 0.125)
+        ds = p * (d_scr[buf, at_rows(base, ch), :] - delta)
         cat = jnp.concatenate([ds.astype(BF), p.astype(BF)], axis=1)
         cols = [lst[r, base + t] for t in range(ch)]
         rhs = jnp.concatenate([kv[at_block(j), :] for j in cols], axis=0)
@@ -113,14 +113,17 @@
 
         oq, l, d, mf = sweep(r, body, (jnp.zeros((2 * BLOCK, BLOCK), F32), zero, zero, low))
         ot[i] = oq[BLOCK:, :].T[HD:].astype(BF)
-        dproj[at_block(i), 0:BLOCK] = oq[:BLOCK, :].astype(BF)
+        dproj[at_block(i), 0:BLOCK] = (oq[:BLOCK, :] * 0.125).astype(BF)
         linv, delta = close(l, d)
         return linv, delta, mf
 
     lax.fori_loop(0, NB, row, (*close(l0, d0), m1))
 
+    lane = lax.broadcasted_iota(jnp.int32, (1, BLOCK), 1)
+    key_scale = jnp.where(lane < HD, 0.125, 1.0).astype(F32)
+
     def fin(i, _):
-        a = acc[at_block(i), :].astype(BF)
+        a = (acc[at_block(i), :] * key_scale).astype(BF)
         q = dproj[at_block(i), 0:BLOCK]
         dproj[at_block(i), :] = jnp.concatenate([q[:, :HD], a], axis=1)
         return 0
@@ -215,7 +218,7 @@
 
 def gather_kernel(
     x, w_hbm, g_hbm, pairs_hbm,
-    xall, b1, b2, kv, lst,
+    xall, b1, b2, kv, lst, wout,
     w, g, pairs, xg, gsend, grecv, sz, rz, sy, ry, sg, rg, lx, ll, hop,
 ):
     s, y, z = ring_place()
@@ -228,11 +231,13 @@
     load_w = pltpu.make_async_copy(w_hbm.at[pl.ds(HD, BLOCK)], w.at[pl.ds(0, BLOCK)], ll.at[2])
     load_q = pltpu.make_async_copy(w_hbm.at[pl.ds(0, HD)], w.at[pl.ds(BLOCK, HD)], ll.at[4])
     load_p = pltpu.make_async_copy(pairs_hbm, pairs, ll.at[3])
+    pass_w = pltpu.make_async_copy(w_hbm, wout, ll.at[5])
     load.start()
     load_g.start()
     load_w.start()
     load_q.start()
     load_p.start()
+    pass_w.start()
     near = [up, down, across]
     greet(near)
 
@@ -331,6 +336,7 @@
         sent.append(c)
     grecv[s] = gsend[s]
     load_p.wait()
+    pass_w.wait()
     lst[...] = row_lists(pairs[...])
 
     def place(t, _):
@@ -398,9 +404,10 @@
             jax.ShapeDtypeStruct((NB, 2 * BLOCK, BLOCK), BF),
             jax.ShapeDtypeStruct((n, BLOCK), BF),
             jax.ShapeDtypeStruct((NB, BLOCK), jnp.int32),
+            jax.ShapeDtypeStruct((3 * HD, D), BF),
         ),
         in_specs=[hbm, hbm, hbm, hbm],
-        out_specs=(anyw, vm, vm, vm, vm),
+        out_specs=(anyw, vm, vm, vm, vm, vm),
         scratch_shapes=[
             pltpu.VMEM((3 * HD, D), BF),
             pltpu.VMEM((BLOCK, D), BF),
@@ -415,7 +422,7 @@
             sem((NB - 1,)),
             sem((NB - 1,)),
             sem((NB,)),
-            sem((5,)),
+            sem((6,)),
             pltpu.SemaphoreType.REGULAR((4,)),
         ],
         compiler_params=pltpu.CompilerParams(
@@ -445,8 +452,17 @@
     def xpeer(d):
         return {"clus": lax.rem(cx + d, NX) * (NY * CORES) + ch * CORES + cc}
 
-    def hpeer(d):
-        return {"clus": cx * (NY * CORES) + lax.rem(ch + d, NY) * CORES + cc}
+    def hplace(h):
+        return {"clus": cx * (NY * CORES) + h * CORES + cc}
+
+    odd = lax.rem(ch, 2)
+    hpair = [hplace(ch + 1 - 2 * odd), hplace(lax.rem(ch + NY - 1 + 2 * odd, NY))]
+
+    def turn(t, _):
+        at = pl.ds(pl.multiple_of(t * BLOCK, BLOCK), BLOCK)
+        v = jnp.concatenate([dproj[at, :].astype(F32), jnp.zeros((BLOCK, HD), F32)], axis=1)
+        dt[:, at] = v.T[: 3 * HD].astype(BF)
+        return 0
 
     def terms():
         def step(t, _):
@@ -456,12 +472,13 @@
 
         lax.fori_loop(0, D // 256, step, 0)
         arecv[s] = ot[s]
+        lax.fori_loop(0, NB, turn, 0)
 
     greet(
         [{"seq": lax.rem(s + d, NB)} for d in range(1, NB)]
         + [sib]
         + [xpeer(d) for d in range(1, NX)]
-        + [hpeer(d) for d in range(1, NY)],
+        + hpair,
         terms,
     )
 
@@ -542,12 +559,6 @@
         to = lax.rem(s + d, NB)
         go(rcopy(ot.at[to], arecv.at[s], sa.at[d - 1], ra.at[d - 1], {"seq": to}))
 
-    def turn(t, _):
-        at = pl.ds(pl.multiple_of(t * BLOCK, BLOCK), BLOCK)
-        v = jnp.concatenate([dproj[at, :].astype(F32), jnp.zeros((BLOCK, HD), F32)], axis=1)
-        dt[:, at] = v.T[: 3 * HD].astype(BF)
-        return 0
-
     def wstep(t, _):
         at = pl.ds(pl.multiple_of(t * 256, 256), 256)
         dwf[:, at] = jnp.dot(dt[...], xv[:, at], preferred_element_type=F32)
@@ -559,7 +570,6 @@
     wide = D // NX
 
     def stage0():
-        lax.fori_loop(0, NB, turn, 0)
         lax.fori_loop(0, D // 256, wstep, 0)
         cs[...] = dwf[other, :].astype(BF)
         go(rcopy(cs, cr, sc.at[0], rc.at[0], sib))
@@ -578,16 +588,20 @@
             frm = lax.rem(cx + NX - d, NX)
             rcopy(xs.at[cx], xr.at[frm], sx.at[d - 1], rx.at[d - 1], xpeer(d)).wait_recv()
         v = xr[0].astype(F32) + xr[1].astype(F32) + xr[2].astype(F32) + xr[3].astype(F32)
-        hs[...] = v.astype(BF)
-        hr[ch] = v.astype(BF)
-        for d in range(1, NY):
-            go(rcopy(hs, hr.at[ch], sh.at[d - 1], rh.at[d - 1], hpeer(d)))
+        hs[0] = v.astype(BF)
+        go(hmsg(0))
+
+    def hmsg(t):
+        return rcopy(hs.at[t], hr.at[t], sh.at[t], rh.at[t], hpair[t])
+
+    def stage3a():
+        hmsg(0).wait_recv()
+        hs[1] = (hs[0].astype(F32) + hr[0].astype(F32)).astype(BF)
+        go(hmsg(1))
 
     def stage3():
-        for d in range(1, NY):
-            frm = lax.rem(ch + NY - d, NY)
-            rcopy(hs, hr.at[frm], sh.at[d - 1], rh.at[d - 1], hpeer(d)).wait_recv()
-        v = hr[0].astype(F32) + hr[1].astype(F32) + hr[2].astype(F32) + hr[3].astype(F32)
+        hmsg(1).wait_recv()
+        v = hs[1].astype(F32) + hr[1].astype(F32)
         fs[...] = v.astype(BF)
         fo[cx] = v.astype(BF)
         for d in range(1, NX):
@@ -636,6 +650,7 @@
     ysend(-1)
     stage2()
     asteps(2)
+    stage3a()
     for flow in (4, 5, 2, 3):
         zstep(flow, 3)
     ysend(0)
@@ -689,8 +704,8 @@
             vmem((hrow, D), BF),
             vmem((NX, hrow, wide), BF),
             vmem((NX, hrow, wide), BF),
-            vmem((hrow, wide), BF),
-            vmem((NY, hrow, wide), BF),
+            vmem((2, hrow, wide), BF),
+            vmem((2, hrow, wide), BF),
             vmem((hrow, wide), BF),
             vmem((NX, hrow, wide), BF),
             vmem((NX, hrow, wide), BF),
@@ -704,8 +719,8 @@
             sem((2,)),
             sem((NX - 1,)),
             sem((NX - 1,)),
-            sem((NY - 1,)),
-            sem((NY - 1,)),
+            sem((2,)),
+            sem((2,)),
             sem((NX - 1,)),
             sem((NX - 1,)),
         ],
@@ -744,9 +759,9 @@
 def local(node_feats, qkv_weight, block_pairs, grad_out):
     operands = (node_feats, qkv_weight, grad_out, jnp.transpose(block_pairs[0]))
     held = [pltpu.with_memory_space_constraint(t, pltpu.HBM) for t in operands]
-    xall, b1, b2, kv, lst = gather(*held)
+    xall, b1, b2, kv, lst, w = gather(*held)
     ot, dproj = attention(lst, b1, b2, kv)
-    return put(*scatter(dproj, qkv_weight, ot, xall.reshape(NB * BLOCK, D)))
+    return put(*scatter(dproj, w, ot, xall.reshape(NB * BLOCK, D)))
 
 
 def solution(mesh):

time: 118 us -> 118 us (level)
    pallas_call x1, Pallas kernels: 44.9 us -> 46.1 us  [scatter(): pl.pallas_call(scatter_kernel, out_shape=(jax.ShapeDtypeStruct((1, BLOCK,...]
where the time goes in v6:
time: 118 us; the launch traced here: 117 us
  Pallas kernels  116 us (98%)
    pallas_call x1, Pallas kernels, gather(): pl.pallas_call(gather_kernel, out_shape=(jax.ShapeDtypeStruct((NB, BLOCK,...  49.6 us
    pallas_call x1, Pallas kernels, scatter(): pl.pallas_call(scatter_kernel, out_shape=(jax.ShapeDtypeStruct((1, BLOCK,...  46.1 us
    pallas_call x1, Pallas kernels, attention(): pl.pallas_call(attn_kernel, out_shape=(jax.ShapeDtypeStruct((NB, HD, BLOC...  19.1 us

profile of v6, /device:TPU:1, one launch (start us, length us, event | category | flops | bytes accessed | tf_op | source)
XLA Modules:
  0.0 116.7 jit_solution(15998685004456727526)
XLA Ops:
  0.6 49.6 %gather_project.1 = (bf16[16,128,1024]{2,1,0:T(8,128)(2,1)S(1)}, bf16[16,128,256]{2,1,0:T(8,128)(2,1)S(1)}, bf16[16,256,128]{2,1,0:T(8,128)(2,1)S(1)}, bf16[2048...) custom-call(bf16[1,128,1024]{2,1,0:T(8,128)(2,1)} %x.1, bf16[192,1024]{1,0:T(8,128)(2,1)} %w_hbm.1, ...), custom_call_target="tpu_custom_call" | custom-call | tf_op jit(solution)/shard_map/gather_project/pallas_call | solution.py:399
  50.3 19.1 %attention.1 = (bf16[16,64,128]{2,1,0:T(8,128)(2,1)S(1)}, bf16[2048,192]{1,0:T(8,128)(2,1)S(1)}) custom-call(s32[16,128]{1,0:T(8,128)S(1)} %get-tuple-element.14.lst, bf16[16,128,256]{2,1,0:T(8,128)(2,1)S(1)} %get-tuple-element.15.b1, bf16[16,256,128]{2,1,0:T(8,128)(2,1)S(1)} %get-tuple-element.16.b2, bf16[2048,128]{1,0:T(8,128)(2,1)S(1)} %get-tuple-element.17.kv), custom_call_target="tpu_custom_call" | custom-call | tf_op jit(solution)/shard_map/attention/pallas_call | solution.py:137
  69.3 46.1 %scatter_reduce.1 = (bf16[1,128,1024]{2,1,0:T(8,128)(2,1)S(1)}, bf16[1,128,1024]{2,1,0:T(8,128)(2,1)S(1)}, f32[192,1024]{1,0:T(8,128)S(1)}) custom-call(bf16[2048,192]{1,0:T(8,128)(2,1)S(1)} %get-tuple-element.18.dproj, bf16[192,1024]{1,0:T(8,128)(2,1)S(1)} %get-tuple-element.19.w, bf16[16,64,128]{2,1,0:T(8,128)(2,1)S(1)} %get-tuple-element.20.ot, ...), custom_call_target="tpu_custom_call" | custom-call | tf_op jit(solution)/shard_map/scatter_reduce/pallas_call | solution.py:685
  115.5 1.1 put.1

commit v7 on v5

--- a/solution.py
+++ b/solution.py
@@ -56,7 +56,7 @@
 
     def gradients(r, base, ch, buf, w2, linv, delta, oq):
         p = s_scr[buf, at_rows(base, ch), :] * linv
-        ds = p * ((d_scr[buf, at_rows(base, ch), :] - delta) * 0.125)
+        ds = p * (d_scr[buf, at_rows(base, ch), :] - delta)
         cat = jnp.concatenate([ds.astype(BF), p.astype(BF)], axis=1)
         cols = [lst[r, base + t] for t in range(ch)]
         rhs = jnp.concatenate([kv[at_block(j), :] for j in cols], axis=0)
@@ -113,14 +113,17 @@
 
         oq, l, d, mf = sweep(r, body, (jnp.zeros((2 * BLOCK, BLOCK), F32), zero, zero, low))
         ot[i] = oq[BLOCK:, :].T[HD:].astype(BF)
-        dproj[at_block(i), 0:BLOCK] = oq[:BLOCK, :].astype(BF)
+        dproj[at_block(i), 0:BLOCK] = (oq[:BLOCK, :] * 0.125).astype(BF)
         linv, delta = close(l, d)
         return linv, delta, mf
 
     lax.fori_loop(0, NB, row, (*close(l0, d0), m1))
 
+    lane = lax.broadcasted_iota(jnp.int32, (1, BLOCK), 1)
+    key_scale = jnp.where(lane < HD, 0.125, 1.0).astype(F32)
+
     def fin(i, _):
-        a = acc[at_block(i), :].astype(BF)
+        a = (acc[at_block(i), :] * key_scale).astype(BF)
         q = dproj[at_block(i), 0:BLOCK]
         dproj[at_block(i), :] = jnp.concatenate([q[:, :HD], a], axis=1)
         return 0
@@ -215,7 +218,7 @@
 
 def gather_kernel(
     x, w_hbm, g_hbm, pairs_hbm,
-    xall, b1, b2, kv, lst,
+    xall, b1, b2, kv, lst, wout,
     w, g, pairs, xg, gsend, grecv, sz, rz, sy, ry, sg, rg, lx, ll, hop,
 ):
     s, y, z = ring_place()
@@ -228,11 +231,13 @@
     load_w = pltpu.make_async_copy(w_hbm.at[pl.ds(HD, BLOCK)], w.at[pl.ds(0, BLOCK)], ll.at[2])
     load_q = pltpu.make_async_copy(w_hbm.at[pl.ds(0, HD)], w.at[pl.ds(BLOCK, HD)], ll.at[4])
     load_p = pltpu.make_async_copy(pairs_hbm, pairs, ll.at[3])
+    pass_w = pltpu.make_async_copy(w_hbm, wout, ll.at[5])
     load.start()
     load_g.start()
     load_w.start()
     load_q.start()
     load_p.start()
+    pass_w.start()
     near = [up, down, across]
     greet(near)
 
@@ -331,6 +336,7 @@
         sent.append(c)
     grecv[s] = gsend[s]
     load_p.wait()
+    pass_w.wait()
     lst[...] = row_lists(pairs[...])
 
     def place(t, _):
@@ -398,9 +404,10 @@
             jax.ShapeDtypeStruct((NB, 2 * BLOCK, BLOCK), BF),
             jax.ShapeDtypeStruct((n, BLOCK), BF),
             jax.ShapeDtypeStruct((NB, BLOCK), jnp.int32),
+            jax.ShapeDtypeStruct((3 * HD, D), BF),
         ),
         in_specs=[hbm, hbm, hbm, hbm],
-        out_specs=(anyw, vm, vm, vm, vm),
+        out_specs=(anyw, vm, vm, vm, vm, vm),
         scratch_shapes=[
             pltpu.VMEM((3 * HD, D), BF),
             pltpu.VMEM((BLOCK, D), BF),
@@ -415,7 +422,7 @@
             sem((NB - 1,)),
             sem((NB - 1,)),
             sem((NB,)),
-            sem((5,)),
+            sem((6,)),
             pltpu.SemaphoreType.REGULAR((4,)),
         ],
         compiler_params=pltpu.CompilerParams(
@@ -448,6 +455,12 @@
     def hpeer(d):
         return {"clus": cx * (NY * CORES) + lax.rem(ch + d, NY) * CORES + cc}
 
+    def turn(t, _):
+        at = pl.ds(pl.multiple_of(t * BLOCK, BLOCK), BLOCK)
+        v = jnp.concatenate([dproj[at, :].astype(F32), jnp.zeros((BLOCK, HD), F32)], axis=1)
+        dt[:, at] = v.T[: 3 * HD].astype(BF)
+        return 0
+
     def terms():
         def step(t, _):
             at = pl.ds(pl.multiple_of(t * 256, 256), 256)
@@ -456,6 +469,7 @@
 
         lax.fori_loop(0, D // 256, step, 0)
         arecv[s] = ot[s]
+        lax.fori_loop(0, NB, turn, 0)
 
     greet(
         [{"seq": lax.rem(s + d, NB)} for d in range(1, NB)]
@@ -542,12 +556,6 @@
         to = lax.rem(s + d, NB)
         go(rcopy(ot.at[to], arecv.at[s], sa.at[d - 1], ra.at[d - 1], {"seq": to}))
 
-    def turn(t, _):
-        at = pl.ds(pl.multiple_of(t * BLOCK, BLOCK), BLOCK)
-        v = jnp.concatenate([dproj[at, :].astype(F32), jnp.zeros((BLOCK, HD), F32)], axis=1)
-        dt[:, at] = v.T[: 3 * HD].astype(BF)
-        return 0
-
     def wstep(t, _):
         at = pl.ds(pl.multiple_of(t * 256, 256), 256)
         dwf[:, at] = jnp.dot(dt[...], xv[:, at], preferred_element_type=F32)
@@ -559,7 +567,6 @@
     wide = D // NX
 
     def stage0():
-        lax.fori_loop(0, NB, turn, 0)
         lax.fori_loop(0, D // 256, wstep, 0)
         cs[...] = dwf[other, :].astype(BF)
         go(rcopy(cs, cr, sc.at[0], rc.at[0], sib))
@@ -744,9 +751,9 @@
 def local(node_feats, qkv_weight, block_pairs, grad_out):
     operands = (node_feats, qkv_weight, grad_out, jnp.transpose(block_pairs[0]))
     held = [pltpu.with_memory_space_constraint(t, pltpu.HBM) for t in operands]
-    xall, b1, b2, kv, lst = gather(*held)
+    xall, b1, b2, kv, lst, w = gather(*held)
     ot, dproj = attention(lst, b1, b2, kv)
-    return put(*scatter(dproj, qkv_weight, ot, xall.reshape(NB * BLOCK, D)))
+    return put(*scatter(dproj, w, ot, xall.reshape(NB * BLOCK, D)))
 
 
 def solution(mesh):

time: 118 us -> 117 us (level)
  no operation moved by 1% of the time
where the time goes in v7:
time: 117 us; the launch traced here: 116 us
  Pallas kernels  115 us (98%)
    pallas_call x1, Pallas kernels, gather(): pl.pallas_call(gather_kernel, out_shape=(jax.ShapeDtypeStruct((NB, BLOCK,...  49.6 us
    pallas_call x1, Pallas kernels, scatter(): pl.pallas_call(scatter_kernel, out_shape=(jax.ShapeDtypeStruct((1, BLOCK,...  45.8 us
    pallas_call x1, Pallas kernels, attention(): pl.pallas_call(attn_kernel, out_shape=(jax.ShapeDtypeStruct((NB, HD, BLOC...  18.8 us

profile of v7, /device:TPU:1, one launch (start us, length us, event | category | flops | bytes accessed | tf_op | source)
XLA Modules:
  0.0 116.1 jit_solution(18010486170184898090)
XLA Ops:
  0.6 49.6 %gather_project.1 = (bf16[16,128,1024]{2,1,0:T(8,128)(2,1)S(1)}, bf16[16,128,256]{2,1,0:T(8,128)(2,1)S(1)}, bf16[16,256,128]{2,1,0:T(8,128)(2,1)S(1)}, bf16[2048...) custom-call(bf16[1,128,1024]{2,1,0:T(8,128)(2,1)} %x.1, bf16[192,1024]{1,0:T(8,128)(2,1)} %w_hbm.1, ...), custom_call_target="tpu_custom_call" | custom-call | tf_op jit(solution)/shard_map/gather_project/pallas_call | solution.py:399
  50.3 18.8 %attention.1 = (bf16[16,64,128]{2,1,0:T(8,128)(2,1)S(1)}, bf16[2048,192]{1,0:T(8,128)(2,1)S(1)}) custom-call(s32[16,128]{1,0:T(8,128)S(1)} %get-tuple-element.14.lst, bf16[16,128,256]{2,1,0:T(8,128)(2,1)S(1)} %get-tuple-element.15.b1, bf16[16,256,128]{2,1,0:T(8,128)(2,1)S(1)} %get-tuple-element.16.b2, bf16[2048,128]{1,0:T(8,128)(2,1)S(1)} %get-tuple-element.17.kv), custom_call_target="tpu_custom_call" | custom-call | tf_op jit(solution)/shard_map/attention/pallas_call | solution.py:137
  69.1 45.8 %scatter_reduce.1 = (bf16[1,128,1024]{2,1,0:T(8,128)(2,1)S(1)}, bf16[1,128,1024]{2,1,0:T(8,128)(2,1)S(1)}, f32[192,1024]{1,0:T(8,128)S(1)}) custom-call(bf16[2048,192]{1,0:T(8,128)(2,1)S(1)} %get-tuple-element.18.dproj, bf16[192,1024]{1,0:T(8,128)(2,1)S(1)} %get-tuple-element.19.w, bf16[16,64,128]{2,1,0:T(8,128)(2,1)S(1)} %get-tuple-element.20.ot, ...), custom_call_target="tpu_custom_call" | custom-call | tf_op jit(solution)/shard_map/scatter_reduce/pallas_call | solution.py:677
  114.9 1.1 put.1
